TPU v7x, 512 devices: a whole 4x8x8 slice. The times are simulated.
512 devices in a mesh: tok: 16 (over y, core), voc: 32 (over x, z).
Axes of the slice: x: 4, y: 8, z: 8, core: 2. Of those that a mesh axis runs over, the one named last changes fastest.
Arguments:
- hidden: bfloat16 [4096, 2048], P('tok')
- panel: bfloat16 [2048, 8192], P(None, 'voc'), may hold values from -0.25 to 0.25
- in_proj: bfloat16 [2048, 64], replicated, may hold values from -0.125 to 0.125
- out_proj: bfloat16 [8192, 64], P('voc'), may hold values from -6 to 6
- targets: int32 [4096], P('tok'), may hold values from 0 to 8191
- keep: int32 [4096], P('tok'), may hold values 0 or 1
- span_ids: int32 [4096], P('tok'), may hold values from 0 to 511, as said below
- store: bfloat16 [131072, 4096], P(('tok', 'voc')), may hold values from -6 to 6
Outputs:
- hidden_grad: bfloat16 [4096, 2048], P('tok', 'voc')
- scores: float32 [512, 131072], P(None, ('tok', 'voc'))
Inputs may be any that keep to these rules, and one draw needn't show every extreme that they name: `span_ids`: tokens k * 256 to (k + 1) * 256 - 1 hold exactly the spans k * 32 to (k + 1) * 32 - 1 in increasing order, each of one or more tokens.
All inputs are finite; a program needn't handle non-finite values. No bound on the sum of `keep` on one device may be relied on, other than what follows from the above.
Results may differ from a plain program's by a relative error of at most 0.018.
Values may be sent and summed in bfloat16 or wider, within the bound.
No kernel may reach another device: no remote copies, remote signals or barrier semaphores. Data moves between devices by JAX's collectives and lax.ppermute only.
A program may use at most 64 MiB of HBM per device.

v0:
```python
import jax
import jax.numpy as jnp
from jax import lax
from jax.sharding import PartitionSpec as P

RANK = 64
SPAN_DEV = 32


def sent_to_all(array, axis):
    devices = lax.axis_size(axis)
    return lax.all_to_all(
        jnp.broadcast_to(array[None], (devices, *array.shape)), axis, 0, 0, tiled=True
    )


def collected_together(array, axis):
    leaves = jax.tree.leaves(array)
    order = sorted(range(len(leaves)), key=lambda k: -leaves[k].size)
    width = (1, *leaves[order[0]].shape)[-1]
    lines = [
        jnp.pad(leaves[k].reshape(-1), (0, -leaves[k].size % width)).reshape(-1, width)
        for k in order
    ]
    both, at, found = (sent_to_all(jnp.concatenate(lines), axis), 0, {})
    for k, line in zip(order, lines):
        share = both[:, at : at + len(line)].reshape(len(both), -1)
        found[k] = share[:, : leaves[k].size].reshape(-1, *leaves[k].shape)
        at += len(line)
    numbers = iter(range(len(leaves)))
    return jax.tree.map(lambda _: found[next(numbers)], array)


def combined_pairwise(pieces, combine):
    while len(jax.tree.leaves(pieces)[0]) > 1:
        pieces = jax.vmap(combine)(
            *(jax.tree.map(lambda part: part[side::2], pieces) for side in (0, 1))
        )
    return jax.tree.map(lambda part: part[0], pieces)


def merged(array, axis, combine):
    pieces = collected_together(array, axis)
    return combined_pairwise(pieces, combine)


def in_blocks(array, dim, devices):
    lengths = array.shape
    parts = array.reshape(*lengths[:dim], devices, lengths[dim] // devices, *lengths[dim + 1 :])
    return jnp.moveaxis(parts, dim, 0)


def sum_at_owner(array, axis, dim):
    devices = lax.axis_size(axis)
    parts = lax.all_to_all(in_blocks(array, dim, devices), axis, 0, 0, tiled=True)
    return jnp.sum(parts.astype(jnp.float32), axis=0)


def of_everyone(array, axis):
    everything = sent_to_all(array, axis)
    return jnp.sum(everything.astype(jnp.float32), axis=0)


def combine_stats(first, second):
    top = jnp.maximum(first[0], second[0])
    total = first[1] * jnp.exp(first[0] - top) + second[1] * jnp.exp(second[0] - top)
    return (top, total)


def span_sums(member, inner, outer):
    weighted = member[:, :, None] * inner[None, :, :]
    summed = lax.dot_general(
        weighted,
        outer,
        (((1,), (0,)), ((), ())),
        precision=lax.Precision.HIGHEST,
        preferred_element_type=jnp.float32,
    )
    return summed.reshape(member.shape[0], inner.shape[1] * outer.shape[1])


def body(hidden, panel, in_proj, out_proj, targets, keep, span_ids, store):
    panel_cols = panel.shape[1]
    logits = jnp.dot(hidden, panel, preferred_element_type=jnp.float32)
    local_top = jnp.max(logits, axis=1)
    local_total = jnp.sum(jnp.exp(logits - local_top[:, None]), axis=1)
    top, total = merged((local_top, local_total), "voc", combine_stats)
    lse = top + jnp.log(total)
    columns = lax.axis_index("voc") * panel_cols + jnp.arange(panel_cols, dtype=jnp.int32)
    onehot = (targets[:, None] == columns[None, :]).astype(jnp.float32)
    grad = ((jnp.exp(logits - lse[:, None]) - onehot) * keep.astype(jnp.float32)[:, None]).astype(
        jnp.bfloat16
    )
    partial_hidden = lax.dot_general(
        grad, panel, (((1,), (1,)), ((), ())), preferred_element_type=jnp.float32
    )
    hidden_grad = sum_at_owner(partial_hidden.astype(jnp.bfloat16), "voc", 1).astype(jnp.bfloat16)
    inner = jnp.dot(hidden, in_proj, preferred_element_type=jnp.float32)
    outer_part = jnp.dot(grad, out_proj, preferred_element_type=jnp.float32)
    local_span = span_ids - lax.axis_index("tok") * SPAN_DEV
    member = (local_span[None, :] == jnp.arange(SPAN_DEV, dtype=jnp.int32)[:, None]).astype(
        jnp.float32
    )
    outer = of_everyone(outer_part.astype(jnp.bfloat16), "voc").astype(jnp.float32)
    queries = span_sums(member, inner, outer).astype(jnp.bfloat16)
    scores = (
        lax.dot_general(
            lax.all_gather(queries, "tok", axis=0, tiled=True),
            store,
            (((1,), (1,)), ((), ())),
            preferred_element_type=jnp.float32,
        )
        / RANK
    )
    return (hidden_grad, scores)


def solution(mesh):
    placed = (
        P("tok", None),
        P(None, "voc"),
        P(),
        P("voc", None),
        P("tok"),
        P("tok"),
        P("tok"),
        P(("tok", "voc"), None),
    )
    return jax.shard_map(
        body,
        mesh=mesh,
        in_specs=placed,
        out_specs=(P("tok", "voc"), P(None, ("tok", "voc"))),
        check_vma=False,
    )
```

profile of v0, /device:TPU:1, one launch (start us, length us, event | category | flops | bytes accessed | tf_op | source)
XLA Modules:
  0.0 127.9 jit_solution(8398585282720557890)
XLA Ops:
  7.2 0.0 copy-start
  7.2 2.2 %fusion.12 = (f32[256]{0:T(256)S(1)}, f32[256,256]{0,1:T(8,128)S(1)}) fusion(bf16[256,2048]{1,0:T(8,128)(2,1)} %param.8, bf16[2048,256]{1,0:T(8,128)(2,1)} %param.9), kind=kOutput, calls=%fused_computation.30 | convolution fusion | flops 268500736 | bytes 2360320 | tf_op jit(solution)/shard_map/dot_general | solution.py:84
  9.4 0.1 exponential_reduce_fusion
  9.5 0.7 broadcast_in_dim.4
  10.2 13.7 %all-to-all-start = ((f32[32,2,256]{2,1,0:T(2,128)}), f32[32,2,256]{2,1,0:T(2,128)S(1)}, u32[]{:S(2)}, u32[]{:S(2)}) async-start(f32[32,2,256]{2,1,0:T(2,128)} %broadcast_in_dim.4), calls=%async_computation | async-start | bytes 131072 | tf_op jit(solution)/shard_map/all_to_all | solution.py:12
  23.9 8.8 %all-to-all-done = f32[32,2,256]{2,1,0:T(2,128)S(1)} async-done(((f32[32,2,256]{2,1,0:T(2,128)}), f32[32,2,256]{2,1,0:T(2,128)S(1)}, u32[]{:S(2)}, u32[]{:S(2)}) %all-to-all-start) | async-done | bytes 65568 | tf_op jit(solution)/shard_map/all_to_all | solution.py:12
  32.7 0.1 fusion.11
  32.8 0.0 copy-start.5
  33.3 1.0 convolution_convert_fusion.1
  34.2 1.2 broadcast_in_dim.5
  35.4 4.7 %all-to-all-start.2 = ((bf16[32,256,64]{1,2,0:T(8,128)(2,1)}), bf16[32,256,64]{1,2,0:T(8,128)(2,1)}, u32[]{:S(2)}, u32[]{:S(2)}) async-start(bf16[32,256,64]{1,2,0:T(8,128)(2,1)} %broadcast_in_dim.5), calls=%async_computation.2 | async-start | bytes 2097152 | tf_op jit(solution)/shard_map/all_to_all | solution.py:12
  40.1 0.0 all-gather.2.cloned.1.call-start
  40.2 1.4 %fusion.13 = f32[256,64]{0,1:T(8,128)S(1)} fusion(bf16[256,2048]{1,0:T(8,128)(2,1)S(1)} %copy-done.1, bf16[2048,64]{0,1:T(8,128)(2,1)} %param.10), kind=kOutput, calls=%fused_computation.31 | convolution fusion | flops 67108864 | bytes 1376256 | tf_op jit(solution)/shard_map/dot_general | solution.py:98
  41.6 22.9 %all-to-all-done.2 = bf16[32,256,64]{1,2,0:T(8,128)(2,1)} async-done(((bf16[32,256,64]{1,2,0:T(8,128)(2,1)}), bf16[32,256,64]{1,2,0:T(8,128)(2,1)}, u32[]{:S(2)}, u32[]{:S(2)}) %all-to-all-start.2) | async-done | bytes 1048608 | tf_op jit(solution)/shard_map/all_to_all | solution.py:12
  64.5 1.4 %convert_reduce_fusion = f32[256,64]{0,1:T(8,128)S(1)} fusion(bf16[32,256,64]{1,2,0:T(8,128)(2,1)} %all-to-all-done.2), kind=kLoop, calls=%fused_computation.1 | loop fusion | flops 1032192 | bytes 1114112 | tf_op jit(solution)/shard_map/reduce_sum | solution.py:61
  65.9 2.6 %fusion.2 = bf16[32,64,64]{2,1,0:T(8,128)(2,1)} fusion(f32[256,64]{0,1:T(8,128)S(1)} %fusion.13, f32[32,256]{1,0:T(8,128)S(1)} %fusion.8, f32[256,64]{0,1:T(8,128)S(1)} %convert_reduce_fusion), kind=kOutput, calls=%fused_computation.4 | convolution fusion | flops 403308544 | bytes 425984 | tf_op jit(solution)/shard_map/dot_general | solution.py:72
  68.5 2.2 %convert_element_type.41 = bf16[32,4096]{1,0:T(8,128)(2,1)} reshape(bf16[32,64,64]{2,1,0:T(8,128)(2,1)} %fusion.2) | data formatting | bytes 524288 | tf_op jit(solution)/shard_map/convert_element_type | solution.py:105
  70.7 0.0 all-gather.2.cloned.1.call-update
  70.7 1.5 %convolution_convert_fusion = bf16[256,2048]{1,0:T(8,128)(2,1)} fusion(bf16[2048,256]{1,0:T(8,128)(2,1)S(1)} %copy-done.2, f32[256,256]{0,1:T(8,128)S(1)} %get-tuple-element.13, f32[256]{0:T(256)S(1)} %convert_element_type.34, s32[256]{0:T(256)S(1)} %copy-done.3, f32[256]{0:T(256)S(1)} %bitcast.24, s32[256]{0:T(256)S(1)} %iota_add_fusion), kind=kOutput, calls=%fused_computation | convolution fusion | flops 269352960 | bytes 2363392 | tf_op jit(solution)/shard_map/dot_general | solution.py:94
  72.3 2.3 %copy.14 = bf16[256,2048]{0,1:T(8,128)(2,1)} copy(bf16[256,2048]{1,0:T(8,128)(2,1)} %convolution_convert_fusion) | data formatting | bytes 2097152 | tf_op jit(solution)/shard_map/convert_element_type | solution.py:97
  74.5 32.7 %all_to_all.15 = bf16[32,256,64]{1,2,0:T(8,128)(2,1)S(1)} all-to-all(bf16[32,256,64]{1,2,0:T(8,128)(2,1)} %bitcast.21), channel_id=1, replica_groups=mesh['tok'=16,'voc'=32] {'voc'}, dimensions={0} | all-to-all | bytes 2097152 | tf_op jit(solution)/shard_map/all_to_all | solution.py:55
  107.2 0.8 reduce_sum.31
  108.0 8.8 %all-gather.2.cloned.1.call-done = bf16[512,4096]{1,0:T(8,128)(2,1)} async-done(((bf16[32,4096]{1,0:T(8,128)(2,1)}), bf16[512,4096]{1,0:T(8,128)(2,1)}) %all-gather.2.cloned.1.call-update) | async-done | bytes 4194320 | tf_op jit(solution)/shard_map/all_gather | solution.py:108
  116.8 4.3 %convolution_multiply_fusion = f32[512,256]{1,0:T(8,128)} fusion(bf16[512,4096]{1,0:T(8,128)(2,1)} %all-gather.2.cloned.1.call-done, bf16[256,4096]{1,0:T(8,128)(2,1)S(1)} %copy-done), kind=kOutput, calls=%fused_computation.5 | convolution fusion | flops 1073872896 | bytes 6815744 | tf_op jit(solution)/shard_map/dot_general | solution.py:107
  (37 shorter events, 0.4 us)
Async XLA Ops:
  7.2 109.6 %copy-start = (bf16[256,4096]{1,0:T(8,128)(2,1)S(1)}, bf16[256,4096]{1,0:T(8,128)(2,1)}, u32[]{:S(2)}) copy-start(bf16[256,4096]{1,0:T(8,128)(2,1)} %param.15) | copy-start | bytes 6291460
  7.2 16.7 %copy-start.4 = (s32[256]{0:T(256)S(1)}, s32[256]{0:T(256)}, u32[]{:S(2)}) copy-start(s32[256]{0:T(256)} %param.13) | copy-start | bytes 3076
  7.2 26.1 %copy-start.3 = (s32[256]{0:T(256)S(1)}, s32[256]{0:T(256)}, u32[]{:S(2)}) copy-start(s32[256]{0:T(256)} %param.12) | copy-start | bytes 3076
  10.2 22.6 %all-to-all-start = ((f32[32,2,256]{2,1,0:T(2,128)}), f32[32,2,256]{2,1,0:T(2,128)S(1)}, u32[]{:S(2)}, u32[]{:S(2)}) async-start(f32[32,2,256]{2,1,0:T(2,128)} %broadcast_in_dim.4), calls=%async_computation | async-start | bytes 131072 | tf_op jit(solution)/shard_map/all_to_all | solution.py:12
  32.8 7.3 %copy-start.5 = (s32[256]{0:T(256)S(1)}, s32[256]{0:T(256)}, u32[]{:S(2)}) copy-start(s32[256]{0:T(256)} %param.14) | copy-start | bytes 3076
  32.8 7.4 %copy-start.1 = (bf16[256,2048]{1,0:T(8,128)(2,1)S(1)}, bf16[256,2048]{1,0:T(8,128)(2,1)}, u32[]{:S(2)}) copy-start(bf16[256,2048]{1,0:T(8,128)(2,1)} %param.8) | copy-start | bytes 3145732
  35.4 29.1 %all-to-all-start.2 = ((bf16[32,256,64]{1,2,0:T(8,128)(2,1)}), bf16[32,256,64]{1,2,0:T(8,128)(2,1)}, u32[]{:S(2)}, u32[]{:S(2)}) async-start(bf16[32,256,64]{1,2,0:T(8,128)(2,1)} %broadcast_in_dim.5), calls=%async_computation.2 | async-start | bytes 2097152 | tf_op jit(solution)/shard_map/all_to_all | solution.py:12
  40.1 76.7 %all-gather.2.cloned.1.call-start = ((), (), s32[]{:S(2)}) async-start(), calls=%async_computation.3 | async-start | bytes 4456448 | tf_op jit(solution)/shard_map/all_gather | solution.py:108
  41.6 29.1 %copy-start.2 = (bf16[2048,256]{1,0:T(8,128)(2,1)S(1)}, bf16[2048,256]{1,0:T(8,128)(2,1)}, u32[]{:S(2)}) copy-start(bf16[2048,256]{1,0:T(8,128)(2,1)} %param.9) | copy-start | bytes 3145732
Sparse Core Ops, SparseCore 0:
  70.8 45.9 all-gather.1
where the time goes:
time: 128 us
  waiting for transfers between devices  40.6 us (32%)
  blocking collectives  32.7 us (26%)
  starting transfers between devices  18.4 us (14%)
  between operations  14.2 us (11%)
  matrix products  13 us (10%)
  local copies, waits for them, and re-layouts  6.66 us (5%)
  other arithmetic  2.33 us (2%)
    all_to_all x1, blocking collectives, sum_at_owner(): lax.all_to_all(in_blocks(array, dim, devices), axis, 0, 0, tiled=True)  32.7 us
    all_to_all x2, waiting for transfers between devices, sent_to_all(): lax.all_to_all(jnp.broadcast_to(array[None], (devices, *array.shape)), ax...  31.8 us
    all_to_all x2, starting transfers between devices, sent_to_all(): lax.all_to_all(jnp.broadcast_to(array[None], (devices, *array.shape)), ax...  18.4 us
    all_gather x1, waiting for transfers between devices, body(): lax.all_gather(queries, 'tok', axis=0, tiled=True)  8.82 us
    dot_general x1, matrix products, body(): lax.dot_general(lax.all_gather(queries, 'tok', axis=0, tiled=True), store...  4.26 us
    dot_general x1, matrix products, span_sums(): lax.dot_general(weighted, outer, (((1,), (0,)), ((), ())), precision=lax....  2.58 us
  transfers between devices with their start and end apart: 3, of which 3 were waited for; matrix products, arithmetic and copies ran while one was open for 5% of the time, Pallas kernels for 0%

commit v1 on v0

v1 whole, which is shorter than its diff:
```python
import functools

import jax
import jax.numpy as jnp
from jax import lax
from jax.experimental import pallas as pl
from jax.experimental.pallas import tpu as pltpu
from jax.sharding import PartitionSpec as P

RANK = 64
SPAN_DEV = 32
LOW = -1e30
F32 = jnp.float32
BF16 = jnp.bfloat16
LANES_BOTH = (((1,), (1,)), ((), ()))


def call(kernel, out_shape, **kw):
    return pl.pallas_call(kernel, out_shape=out_shape, **kw)


def vmem(n):
    return [pl.BlockSpec(memory_space=pltpu.VMEM)] * n


def logits_kernel(steps, base_ref, hid_ref, pan_ref, inp_ref, outp_ref, tgt_ref, span_ref,
                  logit_ref, msg_ref, inner_ref, acc, acc_in, rows):
    step = pl.program_id(0)
    part = jnp.dot(hid_ref[...], pan_ref[...], preferred_element_type=F32)
    part_in = lax.dot_general(inp_ref[...], hid_ref[...], LANES_BOTH, preferred_element_type=F32)

    @pl.when(step == 0)
    def _():
        acc[...] = part
        acc_in[...] = part_in

    @pl.when(step > 0)
    def _():
        acc[...] += part
        acc_in[...] += part_in

    @pl.when(step == steps - 1)
    def _():
        tokens = acc.shape[0]
        inner_ref[0:RANK, :] = acc_in[...].astype(BF16)
        inner_ref[RANK:, :] = jnp.broadcast_to(span_ref[...], (16, tokens)).astype(F32).astype(BF16)
        logit = acc[...].T
        logit_ref[...] = logit
        cols = lax.broadcasted_iota(jnp.int32, logit.shape, 0)
        hot = cols == tgt_ref[...] - base_ref[0]
        others = jnp.where(hot, LOW, logit)
        top = jnp.max(others, axis=0, keepdims=True)
        weight = jnp.exp(others - top)
        total = jnp.sum(weight, axis=0, keepdims=True)
        own = jnp.max(jnp.where(hot, logit, LOW), axis=0, keepdims=True)
        proj = outp_ref[...]
        rows[0:RANK, :] = jnp.dot(proj, weight.astype(BF16), preferred_element_type=F32)
        rows[RANK:, :] = jnp.dot(proj, hot.astype(F32).astype(BF16), preferred_element_type=F32)
        stats = jnp.concatenate([top, total, own], axis=0)
        devices = msg_ref.shape[0]
        share = RANK // devices
        for w in range(devices):
            msg_ref[w, 0:3, :] = stats
            msg_ref[w, 3 : 3 + share, :] = rows[share * w : share * (w + 1), :]
            msg_ref[w, 3 + share : 3 + 2 * share, :] = rows[RANK + share * w : RANK + share * (w + 1), :]
            msg_ref[w, 3 + 2 * share :, :] = jnp.zeros((5 - 2 * share, tokens), F32)


def combine_kernel(got_ref, keep_ref, out_ref, lse_ref, coef):
    devices = got_ref.shape[0]
    tops = got_ref[:, 0, :]
    totals = got_ref[:, 1, :]
    own = jnp.max(got_ref[:, 2, :], axis=0, keepdims=True)
    top = jnp.maximum(jnp.max(tops, axis=0, keepdims=True), own)
    scale = jnp.exp(tops - top)
    rest = jnp.sum(scale * totals, axis=0, keepdims=True)
    total = rest + jnp.exp(own - top)
    lse_ref[...] = top + jnp.log(total)
    keep = keep_ref[...].astype(F32)
    coef[...] = scale * (keep / total)
    gone = keep * (rest / total)
    part = jnp.zeros((2, top.shape[1]), F32)
    hot = jnp.zeros((2, top.shape[1]), F32)
    for v in range(devices):
        part += coef[v : v + 1, :] * got_ref[v, 3:5, :]
        hot += got_ref[v, 5:7, :]
    outer = (part - gone * hot).astype(BF16)
    out_ref[...] = jnp.broadcast_to(outer[None], out_ref.shape)


def scores_kernel(outer_ref, inner_ref, store_ref, out_ref, lhs, sums, query):
    groups = outer_ref.shape[0]
    tokens = outer_ref.shape[2]

    def group(k, carry):
        span = inner_ref[k, RANK : RANK + 1, :].astype(F32)
        block = jnp.floor(span * 0.125)
        row = span - 8.0 * block
        eight = (row == lax.broadcasted_iota(jnp.int32, (8, tokens), 0).astype(F32)).astype(F32)
        inner = inner_ref[k, 0:RANK, :].astype(F32)
        lhs[...] = (inner[:, None, :] * eight[None]).reshape(RANK * 8, tokens).astype(BF16)
        outer = outer_ref[k].astype(F32)
        right = jnp.concatenate(
            [outer * (block == float(j)).astype(F32) for j in range(4)], axis=0
        ).astype(BF16)
        sums[...] = lax.dot_general(lhs[...], right, LANES_BOTH, preferred_element_type=F32)
        for quad in range(RANK // 4):
            rows = [sums[pl.ds((4 * quad + i) * 8, 8), :] for i in range(4)]
            for j in range(0, 4, 2):
                both = [
                    jnp.concatenate([x[:, RANK * jj : RANK * (jj + 1)] for x in rows], axis=1)
                    for jj in (j, j + 1)
                ]
                query[pl.ds(pl.multiple_of(k * SPAN_DEV + 8 * j, 16), 16), 256 * quad : 256 * (quad + 1)] = (
                    jnp.concatenate(both, axis=0).astype(BF16)
                )
        return carry

    lax.fori_loop(0, groups, group, 0)
    out_ref[...] = lax.dot_general(
        query[...], store_ref[...], LANES_BOTH, preferred_element_type=F32
    ) * (1.0 / RANK)


def body(hidden, panel, in_proj, out_proj, targets, keep, span_ids, store):
    tokens, width = hidden.shape
    cols = panel.shape[1]
    devices = lax.axis_size("voc")
    share = width // devices
    base = lax.axis_index("voc") * cols
    local_span = span_ids - lax.axis_index("tok") * SPAN_DEV
    steps = 4
    piece = width // steps
    one = lambda i, b: (0, 0)
    logit, msg, inner = call(
        functools.partial(logits_kernel, steps),
        (
            jax.ShapeDtypeStruct((cols, tokens), F32),
            jax.ShapeDtypeStruct((devices, 8, tokens), F32),
            jax.ShapeDtypeStruct((RANK + 16, tokens), BF16),
        ),
        grid_spec=pltpu.PrefetchScalarGridSpec(
            num_scalar_prefetch=1,
            grid=(steps,),
            in_specs=[
                pl.BlockSpec((tokens, piece), lambda i, b: (0, i)),
                pl.BlockSpec((piece, cols), lambda i, b: (i, 0)),
                pl.BlockSpec((RANK, piece), lambda i, b: (0, i)),
                pl.BlockSpec((RANK, cols), one),
                pl.BlockSpec((1, tokens), one),
                pl.BlockSpec((1, tokens), one),
            ],
            out_specs=[
                pl.BlockSpec((cols, tokens), one),
                pl.BlockSpec((devices, 8, tokens), lambda i, b: (0, 0, 0)),
                pl.BlockSpec((RANK + 16, tokens), one),
            ],
            scratch_shapes=[
                pltpu.VMEM((tokens, cols), F32),
                pltpu.VMEM((RANK, tokens), F32),
                pltpu.VMEM((2 * RANK, tokens), F32),
            ],
        ),
        name="logits",
    )(base[None], hidden, panel, in_proj.T, out_proj.T, targets[None], local_span[None])
    with jax.named_scope("stats_move"):
        got = lax.all_to_all(msg, "voc", 0, 0, tiled=True)
    with jax.named_scope("inner_move"):
        all_inner = lax.all_gather(inner, "tok", axis=0)
    got, all_inner = lax.optimization_barrier((got, all_inner))
    outer, lse = call(
        combine_kernel,
        (
            jax.ShapeDtypeStruct((devices, 2, tokens), BF16),
            jax.ShapeDtypeStruct((1, tokens), F32),
        ),
        in_specs=vmem(2),
        out_specs=tuple(vmem(2)),
        scratch_shapes=[pltpu.VMEM((devices, tokens), F32)],
        name="combine",
    )(got, keep[None])
    with jax.named_scope("outer_move"):
        outer = lax.all_to_all(outer, "voc", 0, 0, tiled=True)
    with jax.named_scope("grad"):
        ids = base + lax.broadcasted_iota(jnp.int32, (cols, tokens), 0)
        onehot = (ids == targets[None]).astype(F32)
        grad = ((jnp.exp(logit - lse) - onehot) * keep.astype(F32)[None]).astype(BF16)
        partial = jnp.dot(panel, grad, preferred_element_type=F32).astype(BF16)
    partial = partial.reshape(devices, share, tokens)
    outer, partial = lax.optimization_barrier((outer, partial))
    with jax.named_scope("hidden_move"):
        parts = lax.all_to_all(partial, "voc", 0, 0, tiled=True)
    with jax.named_scope("gather_move"):
        all_outer = lax.all_gather(outer.reshape(RANK, tokens), "tok", axis=0)
    groups = all_outer.shape[0]
    scores = call(
        scores_kernel,
        jax.ShapeDtypeStruct((groups * SPAN_DEV, store.shape[0]), F32),
        in_specs=vmem(3),
        out_specs=vmem(1)[0],
        scratch_shapes=[
            pltpu.VMEM((RANK * 8, tokens), BF16),
            pltpu.VMEM((RANK * 8, RANK * 4), F32),
            pltpu.VMEM((groups * SPAN_DEV, RANK * RANK), BF16),
        ],
        name="scores",
    )(all_outer, all_inner, store)
    hidden_grad = jnp.sum(parts.astype(F32), axis=0).astype(BF16).T
    return (hidden_grad, scores)


def solution(mesh):
    placed = (
        P("tok", None),
        P(None, "voc"),
        P(),
        P("voc", None),
        P("tok"),
        P("tok"),
        P("tok"),
        P(("tok", "voc"), None),
    )
    return jax.shard_map(
        body,
        mesh=mesh,
        in_specs=placed,
        out_specs=(P("tok", "voc"), P(None, ("tok", "voc"))),
        check_vma=False,
    )
```

time: 128 us -> 96.7 us (0.76)
  waiting for transfers between devices: 40.6 us -> 5.92 us
  Pallas kernels: 0 us -> 15.9 us
  between operations: 14.2 us -> 0.74 us
  matrix products: 13 us -> 1.53 us
  starting transfers between devices: 18.4 us -> 27.1 us
  blocking collectives: 32.7 us -> 40.9 us
  local copies, waits for them, and re-layouts: 6.66 us -> 2.03 us
    all_gather x0 -> x2, blocking collectives: none -> 40.9 us  [the longest x1 21.8 us: body(): all_inner = lax.all_gather(inner, 'tok', axis=0)]
    all_to_all x1 -> x0, blocking collectives: 32.7 us -> none  [sum_at_owner(): lax.all_to_all(in_blocks(array, dim, devices), axis, 0, 0, tiled=True)]
    all_to_all x2 -> x3, waiting for transfers between devices: 31.8 us -> 5.92 us  [the longest x1 5.92 us: body(): outer = lax.all_to_all(outer, 'voc', 0, 0, tiled=True)]
    pallas_call x0 -> x3, Pallas kernels: none -> 15.9 us  [the longest x1 9.8 us: body(): call(scores_kernel, jax.ShapeDtypeStruct((groups * SPAN_DEV, store.shape[...]
    dot_general x6 -> x1, matrix products: 13 us -> 1.53 us  [body(): partial = jnp.dot(panel, grad, preferred_element_type=F32).astype(BF16)]
    all_gather x1 -> x0, waiting for transfers between devices: 8.82 us -> none  [body(): lax.all_gather(queries, 'tok', axis=0, tiled=True)]
    all_to_all x2 -> x3, starting transfers between devices: 18.4 us -> 27.1 us  [the longest x1 13.7 us: body(): got = lax.all_to_all(msg, 'voc', 0, 0, tiled=True)]
    convert_element_type x2 -> x1, local copies, waits for them, and re-layouts: 4.46 us -> 1.3 us  [body(): partial = jnp.dot(panel, grad, preferred_element_type=F32).astype(BF16)]
  transfers between devices with their start and end apart: 3 -> 3, of which waited for: 3 -> 1; matrix products, arithmetic and copies ran while one was open for 5% -> 3% of each run, Pallas kernels for 0% -> 10%
where the time goes in v1:
time: 96.7 us; the launch traced here: 96.3 us
  blocking collectives  40.9 us (42%)
  starting transfers between devices  27.1 us (28%)
  Pallas kernels  15.9 us (16%)
  waiting for transfers between devices  5.92 us (6%)
  other arithmetic  2.11 us (2%)
  local copies, waits for them, and re-layouts  2.03 us (2%)
  matrix products  1.53 us (2%)
    all_gather x1, blocking collectives, body(): all_inner = lax.all_gather(inner, 'tok', axis=0)  21.8 us
    all_gather x1, blocking collectives, body(): all_outer = lax.all_gather(outer.reshape(RANK, tokens), 'tok', axis=0)  19.1 us
    all_to_all x1, starting transfers between devices, body(): got = lax.all_to_all(msg, 'voc', 0, 0, tiled=True)  13.7 us
    pallas_call x1, Pallas kernels, body(): call(scores_kernel, jax.ShapeDtypeStruct((groups * SPAN_DEV, store.shape[...  9.8 us
    all_to_all x1, starting transfers between devices, body(): outer = lax.all_to_all(outer, 'voc', 0, 0, tiled=True)  9.5 us
    all_to_all x1, waiting for transfers between devices, body(): outer = lax.all_to_all(outer, 'voc', 0, 0, tiled=True)  5.92 us
    pallas_call x1, Pallas kernels, body(): call(functools.partial(logits_kernel, steps), (jax.ShapeDtypeStruct((cols...  4.34 us
    all_to_all x1, starting transfers between devices, body(): parts = lax.all_to_all(partial, 'voc', 0, 0, tiled=True)  3.93 us
  transfers between devices with their start and end apart: 3, of which 1 were waited for; matrix products, arithmetic and copies ran while one was open for 3% of the time, Pallas kernels for 10%

profile of v1, /device:TPU:1, one launch (start us, length us, event | category | flops | bytes accessed | tf_op | source)
XLA Modules:
  0.0 96.3 jit_solution(16970651440990935873)
XLA Ops:
  0.6 0.0 copy-start.2
  0.6 0.0 copy-start
  0.7 0.0 copy-start.3
  0.7 1.3 %broadcast_subtract_fusion = s32[256]{0:T(256)} fusion(s32[256]{0:T(256)} %param.14, s32[]{:T(128)S(6)} %mul.15), kind=kLoop, calls=%fused_computation.8 | loop fusion | flops 256 | bytes 2052 | tf_op jit(solution)/shard_map/sub | solution.py:131
  2.0 4.3 %logits.1 = (f32[256,256]{1,0:T(8,128)}, f32[32,8,256]{2,1,0:T(8,128)}, bf16[80,256]{1,0:T(8,128)(2,1)}) custom-call(s32[1]{0:T(128)} %bitcast.base_ref, bf16[256,2048]{1,0:T(8,128)(2,1)} %hid_ref.1, bf16[2048,256]{1,0:T(8,128)(2,1)} %pan_ref.1, bf16[64,2048]{1,0:T(8,128)(2,1)} %bitcast.14, bf16[64,256]{1,0:T(8,128)(2,1)} %bitcast.15, s32[1,256]{1,0:T(1,128)} %bitcast.17, ...), custom_call_target="tpu_custom_call" | custom-call | tf_op jit(solution)/shard_map/logits/pallas_call | solution.py:135
  6.3 13.7 %all-to-all-start = ((f32[32,8,256]{2,1,0:T(8,128)}), f32[32,8,256]{2,1,0:T(8,128)S(1)}, u32[]{:S(2)}, u32[]{:S(2)}) async-start(f32[32,8,256]{2,1,0:T(8,128)} %get-tuple-element.11), calls=%async_computation | async-start | bytes 524288 | tf_op jit(solution)/shard_map/stats_move/all_to_all | solution.py:167
  20.1 0.0 copy-done.3
  20.1 21.8 %all-gather = bf16[1280,256]{1,0:T(8,128)(2,1)} all-gather(bf16[80,256]{1,0:T(8,128)(2,1)} %get-tuple-element.12), channel_id=2, replica_groups=mesh['tok'=16,'voc'=32] {'tok'}, dimensions={0}, use_global_device_ids=true | all-gather | bytes 696320 | tf_op jit(solution)/shard_map/inner_move/all_gather | solution.py:169
  41.9 0.0 all-to-all-done.got_ref
  41.9 0.0 copy-start.1
  41.9 0.7 copy-done.1
  42.6 1.7 %combine.1 = (bf16[32,2,256]{2,1,0:T(2,128)(2,1)}, f32[1,256]{1,0:T(1,128)}) custom-call(f32[32,8,256]{2,1,0:T(8,128)} %copy-done.1, s32[1,256]{1,0:T(1,128)} %bitcast.18), custom_call_target="tpu_custom_call" | custom-call | tf_op jit(solution)/shard_map/combine/pallas_call | solution.py:171
  44.3 9.5 %all-to-all-start.1 = ((bf16[32,2,256]{2,1,0:T(2,128)(2,1)}), bf16[32,2,256]{2,1,0:T(2,128)(2,1)S(1)}, u32[]{:S(2)}, u32[]{:S(2)}) async-start(bf16[32,2,256]{2,1,0:T(2,128)(2,1)} %get-tuple-element.14), calls=%async_computation.1 | async-start | bytes 65536 | tf_op jit(solution)/shard_map/outer_move/all_to_all | solution.py:183
  53.8 0.0 copy-done.2
  53.8 0.0 copy-done
  53.9 1.5 %fusion = bf16[2048,256]{0,1:T(8,128)(2,1)S(1)} fusion(bf16[2048,256]{1,0:T(8,128)(2,1)S(1)} %copy-done, f32[256,256]{1,0:T(8,128)} %get-tuple-element.15, f32[256]{0:T(256)S(1)} %convert_element_type.18, s32[256]{0:T(256)S(1)} %copy-done.2, f32[256]{0:T(256)} %bitcast.20, s32[256]{0:T(256)S(1)} %iota_add_fusion), kind=kOutput, calls=%fused_computation.1 | convolution fusion | flops 269352960 | bytes 2363392 | tf_op jit(solution)/shard_map/grad/dot_general | solution.py:188
  55.4 1.3 %copy.11 = bf16[2048,256]{1,0:T(8,128)(2,1)} copy(bf16[2048,256]{0,1:T(8,128)(2,1)S(1)} %fusion) | data formatting | bytes 2097152 | tf_op jit(solution)/shard_map/grad/convert_element_type | solution.py:188
  56.7 5.9 %all-to-all-done.1 = bf16[32,2,256]{2,1,0:T(2,128)(2,1)S(1)} async-done(((bf16[32,2,256]{2,1,0:T(2,128)(2,1)}), bf16[32,2,256]{2,1,0:T(2,128)(2,1)S(1)}, u32[]{:S(2)}, u32[]{:S(2)}) %all-to-all-start.1) | async-done | bytes 32800 | tf_op jit(solution)/shard_map/outer_move/all_to_all | solution.py:183
  62.6 3.9 %all-to-all-start.2 = ((bf16[32,64,256]{2,1,0:T(8,128)(2,1)}), bf16[32,64,256]{2,1,0:T(8,128)(2,1)S(1)}, u32[]{:S(2)}, u32[]{:S(2)}) async-start(bf16[32,64,256]{2,1,0:T(8,128)(2,1)} %bitcast.9), calls=%async_computation.2 | async-start | bytes 2097152 | tf_op jit(solution)/shard_map/hidden_move/all_to_all | solution.py:192
  66.6 19.1 %all_gather.11.outer_ref = bf16[16,64,256]{2,1,0:T(8,128)(2,1)} all-gather(bf16[1,64,256]{2,1,0:T(8,128)(2,1)S(1)} %reshape.13), channel_id=1, replica_groups=mesh['tok'=16,'voc'=32] {'tok'}, dimensions={0}, use_global_device_ids=true | all-gather | bytes 557056 | tf_op jit(solution)/shard_map/gather_move/all_gather | solution.py:194
  85.7 9.8 %scores.1 = f32[512,256]{1,0:T(8,128)} custom-call(bf16[16,64,256]{2,1,0:T(8,128)(2,1)} %all_gather.11.outer_ref, bf16[16,80,256]{2,1,0:T(8,128)(2,1)} %bitcast.13, bf16[256,4096]{1,0:T(8,128)(2,1)} %store_ref.1), custom_call_target="tpu_custom_call" | custom-call | tf_op jit(solution)/shard_map/scores/pallas_call | solution.py:196
  95.5 0.0 all-to-all-done.2
  95.5 0.8 reduce_sum.12
  (3 shorter events, 0.0 us)
Async XLA Ops:
  0.6 53.2 %copy-start.2 = (s32[256]{0:T(256)S(1)}, s32[256]{0:T(256)}, u32[]{:S(2)}) copy-start(s32[256]{0:T(256)} %param.12) | copy-start | bytes 3076
  0.6 53.2 %copy-start = (bf16[2048,256]{1,0:T(8,128)(2,1)S(1)}, bf16[2048,256]{1,0:T(8,128)(2,1)}, u32[]{:S(2)}) copy-start(bf16[2048,256]{1,0:T(8,128)(2,1)} %pan_ref.1) | copy-start | bytes 3145732
  0.7 19.4 %copy-start.3 = (s32[256]{0:T(256)S(1)}, s32[256]{0:T(256)}, u32[]{:S(2)}) copy-start(s32[256]{0:T(256)} %param.13) | copy-start | bytes 3076
  6.3 35.6 %all-to-all-start = ((f32[32,8,256]{2,1,0:T(8,128)}), f32[32,8,256]{2,1,0:T(8,128)S(1)}, u32[]{:S(2)}, u32[]{:S(2)}) async-start(f32[32,8,256]{2,1,0:T(8,128)} %get-tuple-element.11), calls=%async_computation | async-start | bytes 524288 | tf_op jit(solution)/shard_map/stats_move/all_to_all | solution.py:167
  41.9 0.7 copy-start.1
  44.3 18.3 %all-to-all-start.1 = ((bf16[32,2,256]{2,1,0:T(2,128)(2,1)}), bf16[32,2,256]{2,1,0:T(2,128)(2,1)S(1)}, u32[]{:S(2)}, u32[]{:S(2)}) async-start(bf16[32,2,256]{2,1,0:T(2,128)(2,1)} %get-tuple-element.14), calls=%async_computation.1 | async-start | bytes 65536 | tf_op jit(solution)/shard_map/outer_move/all_to_all | solution.py:183
  62.6 32.9 %all-to-all-start.2 = ((bf16[32,64,256]{2,1,0:T(8,128)(2,1)}), bf16[32,64,256]{2,1,0:T(8,128)(2,1)S(1)}, u32[]{:S(2)}, u32[]{:S(2)}) async-start(bf16[32,64,256]{2,1,0:T(8,128)(2,1)} %bitcast.9), calls=%async_computation.2 | async-start | bytes 2097152 | tf_op jit(solution)/shard_map/hidden_move/all_to_all | solution.py:192

commit v2 on v1

--- a/solution.py
+++ b/solution.py
@@ -7,6 +7,7 @@
 from jax.experimental.pallas import tpu as pltpu
 from jax.sharding import PartitionSpec as P
 
+
 RANK = 64
 SPAN_DEV = 32
 LOW = -1e30
@@ -23,7 +24,7 @@
     return [pl.BlockSpec(memory_space=pltpu.VMEM)] * n
 
 
-def logits_kernel(steps, base_ref, hid_ref, pan_ref, inp_ref, outp_ref, tgt_ref, span_ref,
+def logits_kernel(steps, place_ref, hid_ref, pan_ref, inp_ref, outp_ref, tgt_ref, span_ref,
                   logit_ref, msg_ref, inner_ref, acc, acc_in, rows):
     step = pl.program_id(0)
     part = jnp.dot(hid_ref[...], pan_ref[...], preferred_element_type=F32)
@@ -43,11 +44,12 @@
     def _():
         tokens = acc.shape[0]
         inner_ref[0:RANK, :] = acc_in[...].astype(BF16)
-        inner_ref[RANK:, :] = jnp.broadcast_to(span_ref[...], (16, tokens)).astype(F32).astype(BF16)
+        span = span_ref[...] - place_ref[1] * SPAN_DEV
+        inner_ref[RANK:, :] = jnp.broadcast_to(span, (16, tokens)).astype(F32).astype(BF16)
         logit = acc[...].T
         logit_ref[...] = logit
         cols = lax.broadcasted_iota(jnp.int32, logit.shape, 0)
-        hot = cols == tgt_ref[...] - base_ref[0]
+        hot = cols == tgt_ref[...] - place_ref[0]
         others = jnp.where(hot, LOW, logit)
         top = jnp.max(others, axis=0, keepdims=True)
         weight = jnp.exp(others - top)
@@ -88,16 +90,18 @@
     out_ref[...] = jnp.broadcast_to(outer[None], out_ref.shape)
 
 
-def scores_kernel(outer_ref, inner_ref, store_ref, out_ref, lhs, sums, query):
+def scores_kernel(place_ref, outer_ref, inner_ref, store_ref, out_ref, lhs, sums, query):
     groups = outer_ref.shape[0]
     tokens = outer_ref.shape[2]
 
     def group(k, carry):
-        span = inner_ref[k, RANK : RANK + 1, :].astype(F32)
+        far = place_ref[1] ^ k
+        slot = ((far & 1) << 3) | ((far & 2) << 1) | ((far & 4) >> 1) | ((far & 8) >> 3)
+        span = inner_ref[slot, RANK : RANK + 1, :].astype(F32)
         block = jnp.floor(span * 0.125)
         row = span - 8.0 * block
         eight = (row == lax.broadcasted_iota(jnp.int32, (8, tokens), 0).astype(F32)).astype(F32)
-        inner = inner_ref[k, 0:RANK, :].astype(F32)
+        inner = inner_ref[slot, 0:RANK, :].astype(F32)
         lhs[...] = (inner[:, None, :] * eight[None]).reshape(RANK * 8, tokens).astype(BF16)
         outer = outer_ref[k].astype(F32)
         right = jnp.concatenate(
@@ -122,13 +126,19 @@
     ) * (1.0 / RANK)
 
 
+def doubled(array, bit):
+    there = lax.ppermute(array, "tok", [(k, k ^ bit) for k in range(lax.axis_size("tok"))])
+    return jnp.concatenate([array, there], axis=0)
+
+
 def body(hidden, panel, in_proj, out_proj, targets, keep, span_ids, store):
     tokens, width = hidden.shape
     cols = panel.shape[1]
     devices = lax.axis_size("voc")
     share = width // devices
     base = lax.axis_index("voc") * cols
-    local_span = span_ids - lax.axis_index("tok") * SPAN_DEV
+    me = lax.axis_index("tok")
+    place = jnp.stack([base, me])
     steps = 4
     piece = width // steps
     one = lambda i, b: (0, 0)
@@ -162,11 +172,9 @@
             ],
         ),
         name="logits",
-    )(base[None], hidden, panel, in_proj.T, out_proj.T, targets[None], local_span[None])
-    with jax.named_scope("stats_move"):
-        got = lax.all_to_all(msg, "voc", 0, 0, tiled=True)
-    with jax.named_scope("inner_move"):
-        all_inner = lax.all_gather(inner, "tok", axis=0)
+    )(place, hidden, panel, in_proj.T, out_proj.T, targets[None], span_ids[None])
+    got = lax.all_to_all(msg, "voc", 0, 0, tiled=True)
+    all_inner = doubled(doubled(inner[None], 8), 4)
     got, all_inner = lax.optimization_barrier((got, all_inner))
     outer, lse = call(
         combine_kernel,
@@ -179,24 +187,22 @@
         scratch_shapes=[pltpu.VMEM((devices, tokens), F32)],
         name="combine",
     )(got, keep[None])
-    with jax.named_scope("outer_move"):
-        outer = lax.all_to_all(outer, "voc", 0, 0, tiled=True)
-    with jax.named_scope("grad"):
-        ids = base + lax.broadcasted_iota(jnp.int32, (cols, tokens), 0)
-        onehot = (ids == targets[None]).astype(F32)
-        grad = ((jnp.exp(logit - lse) - onehot) * keep.astype(F32)[None]).astype(BF16)
-        partial = jnp.dot(panel, grad, preferred_element_type=F32).astype(BF16)
+    outer, lse, all_inner = lax.optimization_barrier((outer, lse, all_inner))
+    outer = lax.all_to_all(outer, "voc", 0, 0, tiled=True)
+    ids = base + lax.broadcasted_iota(jnp.int32, (cols, tokens), 0)
+    onehot = (ids == targets[None]).astype(F32)
+    grad = ((jnp.exp(logit - lse) - onehot) * keep.astype(F32)[None]).astype(BF16)
+    partial = jnp.dot(panel, grad, preferred_element_type=F32).astype(BF16)
     partial = partial.reshape(devices, share, tokens)
-    outer, partial = lax.optimization_barrier((outer, partial))
-    with jax.named_scope("hidden_move"):
-        parts = lax.all_to_all(partial, "voc", 0, 0, tiled=True)
-    with jax.named_scope("gather_move"):
-        all_outer = lax.all_gather(outer.reshape(RANK, tokens), "tok", axis=0)
+    all_inner = doubled(doubled(all_inner, 2), 1)
+    outer, partial, all_inner = lax.optimization_barrier((outer, partial, all_inner))
+    parts = lax.all_to_all(partial, "voc", 0, 0, tiled=True)
+    all_outer = lax.all_gather(outer.reshape(RANK, tokens), "tok", axis=0)
     groups = all_outer.shape[0]
     scores = call(
         scores_kernel,
         jax.ShapeDtypeStruct((groups * SPAN_DEV, store.shape[0]), F32),
-        in_specs=vmem(3),
+        in_specs=[pl.BlockSpec(memory_space=pltpu.SMEM)] + vmem(3),
         out_specs=vmem(1)[0],
         scratch_shapes=[
             pltpu.VMEM((RANK * 8, tokens), BF16),
@@ -204,7 +210,7 @@
             pltpu.VMEM((groups * SPAN_DEV, RANK * RANK), BF16),
         ],
         name="scores",
-    )(all_outer, all_inner, store)
+    )(place, all_outer, all_inner, store)
     hidden_grad = jnp.sum(parts.astype(F32), axis=0).astype(BF16).T
     return (hidden_grad, scores)
 
@@ -220,6 +226,7 @@
         P("tok"),
         P(("tok", "voc"), None),
     )
+
     return jax.shard_map(
         body,
         mesh=mesh,

time: 96.7 us -> 111 us (1.15)
  starting transfers between devices: 27.1 us -> 46.3 us
  blocking collectives: 40.9 us -> 22.9 us
  waiting for transfers between devices: 5.92 us -> 16.1 us
  other arithmetic: 2.11 us -> 3.91 us
    all_gather x1 -> x0, blocking collectives: 21.8 us -> none  [body(): all_inner = lax.all_gather(inner, 'tok', axis=0)]
    ppermute x0 -> x4, starting transfers between devices: none -> 19 us  [doubled(): lax.ppermute(array, 'tok', [(k, k ^ bit) for k in range(lax.axis_size('to...]
    ppermute x0 -> x4, waiting for transfers between devices: none -> 8.28 us  [doubled(): lax.ppermute(array, 'tok', [(k, k ^ bit) for k in range(lax.axis_size('to...]
    all_gather x1, blocking collectives: 19.1 us -> 22.9 us  [body(): all_outer = lax.all_gather(outer.reshape(RANK, tokens), 'tok', axis=0)]
    concatenate x0 -> x4, other arithmetic: none -> 2.53 us  [doubled(): return jnp.concatenate([array, there], axis=0)]
    all_to_all x1, waiting for transfers between devices: 5.92 us -> 7.84 us  [body(): outer = lax.all_to_all(outer, 'voc', 0, 0, tiled=True)]
    sub x1 -> x0, other arithmetic: 1.33 us -> none  [body(): local_span = span_ids - lax.axis_index('tok') * SPAN_DEV]
  transfers between devices with their start and end apart: 3 -> 7, of which waited for: 1 -> 4; matrix products, arithmetic and copies ran while one was open for 3% -> 5% of each run, Pallas kernels for 10% -> 9%
where the time goes in v2:
time: 111 us; the launch traced here: 110 us
  starting transfers between devices  46.3 us (42%)
  blocking collectives  22.9 us (21%)
  Pallas kernels  16.8 us (15%)
  waiting for transfers between devices  16.1 us (15%)
  other arithmetic  3.91 us (4%)
  local copies, waits for them, and re-layouts  2.05 us (2%)
  matrix products  1.21 us (1%)
    all_gather x1, blocking collectives, body(): all_outer = lax.all_gather(outer.reshape(RANK, tokens), 'tok', axis=0)  22.9 us
    ppermute x4, starting transfers between devices, doubled(): lax.ppermute(array, 'tok', [(k, k ^ bit) for k in range(lax.axis_size('to...  19 us
    all_to_all x1, starting transfers between devices, body(): got = lax.all_to_all(msg, 'voc', 0, 0, tiled=True)  13.8 us
    pallas_call x1, Pallas kernels, body(): call(scores_kernel, jax.ShapeDtypeStruct((groups * SPAN_DEV, store.shape[...  9.86 us
    all_to_all x1, starting transfers between devices, body(): outer = lax.all_to_all(outer, 'voc', 0, 0, tiled=True)  9.5 us
    ppermute x4, waiting for transfers between devices, doubled(): lax.ppermute(array, 'tok', [(k, k ^ bit) for k in range(lax.axis_size('to...  8.28 us
    all_to_all x1, waiting for transfers between devices, body(): outer = lax.all_to_all(outer, 'voc', 0, 0, tiled=True)  7.84 us
    pallas_call x1, Pallas kernels, body(): call(functools.partial(logits_kernel, steps), (jax.ShapeDtypeStruct((cols...  5.18 us
  transfers between devices with their start and end apart: 7, of which 4 were waited for; matrix products, arithmetic and copies ran while one was open for 5% of the time, Pallas kernels for 9%

profile of v2, /device:TPU:1, one launch (start us, length us, event | category | flops | bytes accessed | tf_op | source)
XLA Modules:
  0.0 110.1 jit_solution(10967128192225302492)
XLA Ops:
  0.6 0.6 pad_add_fusion.place_ref
  1.2 5.2 %logits.1 = (f32[256,256]{1,0:T(8,128)}, f32[32,8,256]{2,1,0:T(8,128)}, bf16[80,256]{1,0:T(8,128)(2,1)}) custom-call(s32[2]{0:T(128)} %pad_add_fusion.place_ref, bf16[256,2048]{1,0:T(8,128)(2,1)} %hid_ref.1, bf16[2048,256]{1,0:T(8,128)(2,1)} %pan_ref.1, bf16[64,2048]{1,0:T(8,128)(2,1)} %bitcast.14, bf16[64,256]{1,0:T(8,128)(2,1)} %bitcast.18, ...), custom_call_target="tpu_custom_call" | custom-call | tf_op jit(solution)/shard_map/logits/pallas_call | solution.py:145
  6.4 13.8 %all-to-all-start = ((f32[32,8,256]{2,1,0:T(8,128)}), f32[32,8,256]{2,1,0:T(8,128)S(1)}, u32[]{:S(2)}, u32[]{:S(2)}) async-start(f32[32,8,256]{2,1,0:T(8,128)} %get-tuple-element.15), calls=%async_computation | async-start | bytes 524288 | tf_op jit(solution)/shard_map/all_to_all | solution.py:176
  20.3 7.5 %collective-permute-start = (bf16[1,80,256]{2,1,0:T(8,128)(2,1)}, bf16[1,80,256]{2,1,0:T(8,128)(2,1)S(1)}, u32[]{:S(2)}, u32[]{:S(2)}) collective-permute-start(bf16[1,80,256]{2,1,0:T(8,128)(2,1)} %bitcast.15), channel_id=1, source_target_pairs={{0,256},{32,288},{64,320},{96,352},{128,384},{160,416},{192,448},{... | collective-permute-start | bytes 122888 | tf_op jit(solution)/shard_map/ppermute | solution.py:130
  27.7 1.9 %collective-permute-done = bf16[1,80,256]{2,1,0:T(8,128)(2,1)S(1)} collective-permute-done((bf16[1,80,256]{2,1,0:T(8,128)(2,1)}, bf16[1,80,256]{2,1,0:T(8,128)(2,1)S(1)}, u32[]{:S(2)}, u32[]{:S(2)}) %collective-permute-start) | collective-permute-done | bytes 40992 | tf_op jit(solution)/shard_map/ppermute | solution.py:130
  29.6 0.8 pad_maximum_fusion.3
  30.4 4.4 %collective-permute-start.1 = (bf16[2,80,256]{2,1,0:T(8,128)(2,1)S(1)}, bf16[2,80,256]{2,1,0:T(8,128)(2,1)S(1)}, u32[]{:S(2)}, u32[]{:S(2)}) collective-permute-start(bf16[2,80,256]{2,1,0:T(8,128)(2,1)S(1)} %pad_maximum_fusion.3), channel_id=1, source_target_pairs={{0,128},{32,160},{64,192},{96,224},{128,0},{160,32},{192,64},{224,... | collective-permute-start | bytes 245768 | tf_op jit(solution)/shard_map/ppermute | solution.py:130
  34.8 2.7 %collective-permute-done.1 = bf16[2,80,256]{2,1,0:T(8,128)(2,1)S(1)} collective-permute-done((bf16[2,80,256]{2,1,0:T(8,128)(2,1)S(1)}, bf16[2,80,256]{2,1,0:T(8,128)(2,1)S(1)}, u32[]{:S(2)}, u32[]{:S(2)}) %collective-permute-start.1) | collective-permute-done | bytes 81952 | tf_op jit(solution)/shard_map/ppermute | solution.py:130
  37.5 0.8 pad_maximum_fusion.2
  38.3 0.0 all-to-all-done.got_ref
  38.3 0.7 copy-done.1
  39.0 1.7 %combine.1 = (bf16[32,2,256]{2,1,0:T(2,128)(2,1)}, f32[1,256]{1,0:T(1,128)}) custom-call(f32[32,8,256]{2,1,0:T(8,128)} %copy-done.1, s32[1,256]{1,0:T(1,128)} %bitcast.21), custom_call_target="tpu_custom_call" | custom-call | tf_op jit(solution)/shard_map/combine/pallas_call | solution.py:179
  40.7 2.3 %collective-permute-start.2 = (bf16[4,80,256]{2,1,0:T(8,128)(2,1)S(1)}, bf16[4,80,256]{2,1,0:T(8,128)(2,1)S(1)}, u32[]{:S(2)}, u32[]{:S(2)}) collective-permute-start(bf16[4,80,256]{2,1,0:T(8,128)(2,1)S(1)} %pad_maximum_fusion.2), channel_id=1, source_target_pairs={{0,64},{32,96},{64,0},{96,32},{128,192},{160,224},{192,128},{224,1... | collective-permute-start | bytes 491528 | tf_op jit(solution)/shard_map/ppermute | solution.py:130
  43.1 3.7 %collective-permute-done.2 = bf16[4,80,256]{2,1,0:T(8,128)(2,1)S(1)} collective-permute-done((bf16[4,80,256]{2,1,0:T(8,128)(2,1)S(1)}, bf16[4,80,256]{2,1,0:T(8,128)(2,1)S(1)}, u32[]{:S(2)}, u32[]{:S(2)}) %collective-permute-start.2) | collective-permute-done | bytes 163872 | tf_op jit(solution)/shard_map/ppermute | solution.py:130
  46.8 4.8 %collective-permute-start.3 = (bf16[8,80,256]{2,1,0:T(8,128)(2,1)S(1)}, bf16[8,80,256]{2,1,0:T(8,128)(2,1)S(1)}, u32[]{:S(2)}, u32[]{:S(2)}) collective-permute-start(bf16[8,80,256]{2,1,0:T(8,128)(2,1)S(1)} %pad_maximum_fusion.1), channel_id=1, source_target_pairs={{0,32},{32,0},{64,96},{96,64},{128,160},{160,128},{192,224},{224,1... | collective-permute-start | bytes 983048 | tf_op jit(solution)/shard_map/ppermute | solution.py:130
  51.7 1.2 %fusion = bf16[2048,256]{0,1:T(8,128)(2,1)S(1)} fusion(bf16[2048,256]{1,0:T(8,128)(2,1)S(1)} %copy-done, f32[256,256]{1,0:T(8,128)S(1)} %copy-done.2, f32[256]{0:T(256)S(1)} %convert_element_type.18, s32[256]{0:T(256)S(1)} %copy-done.3, f32[256]{0:T(256)} %bitcast.23, s32[256]{0:T(256)S(1)} %iota_add_fusion), kind=kOutput, calls=%fused_computation.1 | convolution fusion | flops 269352960 | bytes 2363392 | tf_op jit(solution)/shard_map/dot_general | solution.py:195
  52.9 1.3 %copy.11 = bf16[2048,256]{1,0:T(8,128)(2,1)} copy(bf16[2048,256]{0,1:T(8,128)(2,1)S(1)} %fusion) | data formatting | bytes 2097152 | tf_op jit(solution)/shard_map/convert_element_type | solution.py:195
  54.3 9.5 %all-to-all-start.1 = ((bf16[32,2,256]{2,1,0:T(2,128)(2,1)}), bf16[32,2,256]{2,1,0:T(2,128)(2,1)S(1)}, u32[]{:S(2)}, u32[]{:S(2)}) async-start(bf16[32,2,256]{2,1,0:T(2,128)(2,1)} %get-tuple-element.21), calls=%async_computation.1 | async-start | bytes 65536 | tf_op jit(solution)/shard_map/all_to_all | solution.py:191
  63.8 0.9 pad_maximum_fusion.inner_ref
  64.7 7.8 %all-to-all-done.1 = bf16[32,2,256]{2,1,0:T(2,128)(2,1)S(1)} async-done(((bf16[32,2,256]{2,1,0:T(2,128)(2,1)}), bf16[32,2,256]{2,1,0:T(2,128)(2,1)S(1)}, u32[]{:S(2)}, u32[]{:S(2)}) %all-to-all-start.1) | async-done | bytes 32800 | tf_op jit(solution)/shard_map/all_to_all | solution.py:191
  72.5 3.9 %all-to-all-start.2 = ((bf16[32,64,256]{2,1,0:T(8,128)(2,1)}), bf16[32,64,256]{2,1,0:T(8,128)(2,1)S(1)}, u32[]{:S(2)}, u32[]{:S(2)}) async-start(bf16[32,64,256]{2,1,0:T(8,128)(2,1)} %bitcast.10), calls=%async_computation.2 | async-start | bytes 2097152 | tf_op jit(solution)/shard_map/all_to_all | solution.py:199
  76.5 22.9 %all_gather.3.outer_ref = bf16[16,64,256]{2,1,0:T(8,128)(2,1)} all-gather(bf16[1,64,256]{2,1,0:T(8,128)(2,1)S(1)} %all_gather_reshape.3), channel_id=1, replica_groups=mesh['tok'=16,'voc'=32] {'tok'}, dimensions={0}, use_global_device_ids=true | all-gather | bytes 557056 | tf_op jit(solution)/shard_map/all_gather | solution.py:200
  99.4 9.9 %scores.1 = f32[512,256]{1,0:T(8,128)} custom-call(s32[2]{0:T(128)} %pad_add_fusion.place_ref, bf16[16,64,256]{2,1,0:T(8,128)(2,1)} %all_gather.3.outer_ref, bf16[16,80,256]{2,1,0:T(8,128)(2,1)} %pad_maximum_fusion.inner_ref, bf16[256,4096]{1,0:T(8,128)(2,1)} %store_ref.1), custom_call_target="tpu_custom_call" | custom-call | tf_op jit(solution)/shard_map/scores/pallas_call | solution.py:202
  109.3 0.8 reduce_sum.12
  (15 shorter events, 0.1 us)
Async XLA Ops:
  1.2 50.4 %copy-start.4 = (s32[256]{0:T(256)S(1)}, s32[256]{0:T(256)}, u32[]{:S(2)}) copy-start(s32[256]{0:T(256)} %param.13) | copy-start | bytes 3076
  1.2 50.5 %copy-start = (bf16[2048,256]{1,0:T(8,128)(2,1)S(1)}, bf16[2048,256]{1,0:T(8,128)(2,1)}, u32[]{:S(2)}) copy-start(bf16[2048,256]{1,0:T(8,128)(2,1)} %pan_ref.1) | copy-start | bytes 3145732
  1.2 50.5 %copy-start.3 = (s32[256]{0:T(256)S(1)}, s32[256]{0:T(256)}, u32[]{:S(2)}) copy-start(s32[256]{0:T(256)} %param.12) | copy-start | bytes 3076
  6.4 45.3 %copy-start.2 = (f32[256,256]{1,0:T(8,128)S(1)}, f32[256,256]{1,0:T(8,128)}, u32[]{:S(2)}) copy-start(f32[256,256]{1,0:T(8,128)} %get-tuple-element.22) | copy-start | bytes 786436
  6.4 31.9 %all-to-all-start = ((f32[32,8,256]{2,1,0:T(8,128)}), f32[32,8,256]{2,1,0:T(8,128)S(1)}, u32[]{:S(2)}, u32[]{:S(2)}) async-start(f32[32,8,256]{2,1,0:T(8,128)} %get-tuple-element.15), calls=%async_computation | async-start | bytes 524288 | tf_op jit(solution)/shard_map/all_to_all | solution.py:176
  20.3 9.3 %collective-permute-start = (bf16[1,80,256]{2,1,0:T(8,128)(2,1)}, bf16[1,80,256]{2,1,0:T(8,128)(2,1)S(1)}, u32[]{:S(2)}, u32[]{:S(2)}) collective-permute-start(bf16[1,80,256]{2,1,0:T(8,128)(2,1)} %bitcast.15), channel_id=1, source_target_pairs={{0,256},{32,288},{64,320},{96,352},{128,384},{160,416},{192,448},{... | collective-permute-start | bytes 122888 | tf_op jit(solution)/shard_map/ppermute | solution.py:130
  30.4 7.1 %collective-permute-start.1 = (bf16[2,80,256]{2,1,0:T(8,128)(2,1)S(1)}, bf16[2,80,256]{2,1,0:T(8,128)(2,1)S(1)}, u32[]{:S(2)}, u32[]{:S(2)}) collective-permute-start(bf16[2,80,256]{2,1,0:T(8,128)(2,1)S(1)} %pad_maximum_fusion.3), channel_id=1, source_target_pairs={{0,128},{32,160},{64,192},{96,224},{128,0},{160,32},{192,64},{224,... | collective-permute-start | bytes 245768 | tf_op jit(solution)/shard_map/ppermute | solution.py:130
  38.3 0.7 copy-start.1
  40.7 6.1 %collective-permute-start.2 = (bf16[4,80,256]{2,1,0:T(8,128)(2,1)S(1)}, bf16[4,80,256]{2,1,0:T(8,128)(2,1)S(1)}, u32[]{:S(2)}, u32[]{:S(2)}) collective-permute-start(bf16[4,80,256]{2,1,0:T(8,128)(2,1)S(1)} %pad_maximum_fusion.2), channel_id=1, source_target_pairs={{0,64},{32,96},{64,0},{96,32},{128,192},{160,224},{192,128},{224,1... | collective-permute-start | bytes 491528 | tf_op jit(solution)/shard_map/ppermute | solution.py:130
  46.8 16.9 %collective-permute-start.3 = (bf16[8,80,256]{2,1,0:T(8,128)(2,1)S(1)}, bf16[8,80,256]{2,1,0:T(8,128)(2,1)S(1)}, u32[]{:S(2)}, u32[]{:S(2)}) collective-permute-start(bf16[8,80,256]{2,1,0:T(8,128)(2,1)S(1)} %pad_maximum_fusion.1), channel_id=1, source_target_pairs={{0,32},{32,0},{64,96},{96,64},{128,160},{160,128},{192,224},{224,1... | collective-permute-start | bytes 983048 | tf_op jit(solution)/shard_map/ppermute | solution.py:130
  54.3 18.3 %all-to-all-start.1 = ((bf16[32,2,256]{2,1,0:T(2,128)(2,1)}), bf16[32,2,256]{2,1,0:T(2,128)(2,1)S(1)}, u32[]{:S(2)}, u32[]{:S(2)}) async-start(bf16[32,2,256]{2,1,0:T(2,128)(2,1)} %get-tuple-element.21), calls=%async_computation.1 | async-start | bytes 65536 | tf_op jit(solution)/shard_map/all_to_all | solution.py:191
  72.5 36.8 %all-to-all-start.2 = ((bf16[32,64,256]{2,1,0:T(8,128)(2,1)}), bf16[32,64,256]{2,1,0:T(8,128)(2,1)S(1)}, u32[]{:S(2)}, u32[]{:S(2)}) async-start(bf16[32,64,256]{2,1,0:T(8,128)(2,1)} %bitcast.10), calls=%async_computation.2 | async-start | bytes 2097152 | tf_op jit(solution)/shard_map/all_to_all | solution.py:199

commit v3 on v1

--- a/solution.py
+++ b/solution.py
@@ -15,15 +15,20 @@
 LANES_BOTH = (((1,), (1,)), ((), ()))
 
 
+def resident(array):
+    return pltpu.with_memory_space_constraint(array, pltpu.VMEM)
+
+
 def call(kernel, out_shape, **kw):
-    return pl.pallas_call(kernel, out_shape=out_shape, **kw)
+    room = pltpu.CompilerParams(vmem_limit_bytes=16 << 20)
+    return pl.pallas_call(kernel, out_shape=out_shape, compiler_params=room, **kw)
 
 
 def vmem(n):
     return [pl.BlockSpec(memory_space=pltpu.VMEM)] * n
 
 
-def logits_kernel(steps, base_ref, hid_ref, pan_ref, inp_ref, outp_ref, tgt_ref, span_ref,
+def logits_kernel(steps, hid_ref, pan_ref, inp_ref, outp_ref, tgt_ref, span_ref,
                   logit_ref, msg_ref, inner_ref, acc, acc_in, rows):
     step = pl.program_id(0)
     part = jnp.dot(hid_ref[...], pan_ref[...], preferred_element_type=F32)
@@ -43,11 +48,12 @@
     def _():
         tokens = acc.shape[0]
         inner_ref[0:RANK, :] = acc_in[...].astype(BF16)
-        inner_ref[RANK:, :] = jnp.broadcast_to(span_ref[...], (16, tokens)).astype(F32).astype(BF16)
+        span = (span_ref[...] - lax.axis_index("tok") * SPAN_DEV).astype(F32)
+        inner_ref[RANK:, :] = jnp.broadcast_to(span, (16, tokens)).astype(BF16)
         logit = acc[...].T
         logit_ref[...] = logit
         cols = lax.broadcasted_iota(jnp.int32, logit.shape, 0)
-        hot = cols == tgt_ref[...] - base_ref[0]
+        hot = cols == tgt_ref[...] - lax.axis_index("voc") * acc.shape[1]
         others = jnp.where(hot, LOW, logit)
         top = jnp.max(others, axis=0, keepdims=True)
         weight = jnp.exp(others - top)
@@ -88,38 +94,81 @@
     out_ref[...] = jnp.broadcast_to(outer[None], out_ref.shape)
 
 
-def scores_kernel(outer_ref, inner_ref, store_ref, out_ref, lhs, sums, query):
-    groups = outer_ref.shape[0]
-    tokens = outer_ref.shape[2]
-
-    def group(k, carry):
-        span = inner_ref[k, RANK : RANK + 1, :].astype(F32)
+def grad_kernel(logit_ref, lse_ref, tgt_ref, keep_ref, pan_ref, out_ref, grad):
+    @pl.when(pl.program_id(0) == 0)
+    def _():
+        cols = lax.broadcasted_iota(jnp.int32, logit_ref.shape, 0)
+        hot = cols == tgt_ref[...] - lax.axis_index("voc") * logit_ref.shape[0]
+        soft = jnp.exp(logit_ref[...] - lse_ref[...])
+        keep = keep_ref[...].astype(F32)
+        grad[...] = ((soft - hot.astype(F32)) * keep).astype(BF16)
+
+    out_ref[...] = jnp.dot(pan_ref[...], grad[...], preferred_element_type=F32).astype(BF16)
+
+
+def total_kernel(parts_ref, out_ref):
+    def add(k, total):
+        return total + parts_ref[k].astype(F32)
+
+    devices = parts_ref.shape[0]
+    total = lax.fori_loop(1, devices, add, parts_ref[0].astype(F32), unroll=4)
+    out_ref[...] = total.astype(BF16)
+
+
+def scores_kernel(outer_ref, inner_ref, store_ref, out_ref, query, wide, *sums):
+    groups, rank, tokens = outer_ref.shape
+    half = rank // 2
+    low = lax.broadcasted_iota(jnp.int32, (8, 128), 1) < rank
+    eight = lax.broadcasted_iota(jnp.int32, (8, tokens), 0).astype(F32)
+
+    def multiply(k, even_ref, odd_ref):
+        span = inner_ref[k, rank:, :].astype(F32)
         block = jnp.floor(span * 0.125)
-        row = span - 8.0 * block
-        eight = (row == lax.broadcasted_iota(jnp.int32, (8, tokens), 0).astype(F32)).astype(F32)
-        inner = inner_ref[k, 0:RANK, :].astype(F32)
-        lhs[...] = (inner[:, None, :] * eight[None]).reshape(RANK * 8, tokens).astype(BF16)
-        outer = outer_ref[k].astype(F32)
-        right = jnp.concatenate(
-            [outer * (block == float(j)).astype(F32) for j in range(4)], axis=0
-        ).astype(BF16)
-        sums[...] = lax.dot_general(lhs[...], right, LANES_BOTH, preferred_element_type=F32)
-        for quad in range(RANK // 4):
-            rows = [sums[pl.ds((4 * quad + i) * 8, 8), :] for i in range(4)]
-            for j in range(0, 4, 2):
-                both = [
-                    jnp.concatenate([x[:, RANK * jj : RANK * (jj + 1)] for x in rows], axis=1)
-                    for jj in (j, j + 1)
-                ]
-                query[pl.ds(pl.multiple_of(k * SPAN_DEV + 8 * j, 16), 16), 256 * quad : 256 * (quad + 1)] = (
-                    jnp.concatenate(both, axis=0).astype(BF16)
+        row = (span - 8.0 * block)[0:8, :]
+        mask = (row == eight).astype(F32)
+        for c in (0, 1):
+            wide[c] = inner_ref[k, 0:rank, 128 * c : 128 * (c + 1)].astype(F32)
+        outer = outer_ref[k]
+        shares = []
+        for j in range(4):
+            chosen = (block == float(j)).astype(F32).astype(BF16)
+            shares.append(outer * jnp.concatenate([chosen] * (rank // 16), axis=0))
+        for ref, side, order in ((even_ref, 0, (0, 1, 2, 3)), (odd_ref, 1, (1, 0, 3, 2))):
+            columns = []
+            for c in (0, 1):
+                part = mask[:, 128 * c : 128 * (c + 1)]
+                rows = [wide[c, pl.ds(2 * p + side, 8, stride=0), :] * part for p in range(half)]
+                columns.append(jnp.concatenate(rows, axis=0).astype(BF16))
+            left = jnp.concatenate(columns, axis=1)
+            right = jnp.concatenate([shares[j] for j in order], axis=0)
+            ref[...] = lax.dot_general(left, right, LANES_BOTH, preferred_element_type=F32)
+
+    def arrange(k, even_ref, odd_ref):
+        base = pl.multiple_of(k * SPAN_DEV, SPAN_DEV)
+        for pair in range(half):
+            for c in (0, 1):
+                x = even_ref[8 * pair : 8 * (pair + 1), 128 * c : 128 * (c + 1)]
+                y = odd_ref[8 * pair : 8 * (pair + 1), 128 * c : 128 * (c + 1)]
+                straight = jnp.where(low, x, y)
+                crossed = pltpu.roll(jnp.where(low, y, x), rank, axis=1)
+                query[pl.ds(base + 16 * c, 16), 128 * pair : 128 * (pair + 1)] = (
+                    jnp.concatenate([straight, crossed], axis=0).astype(BF16)
                 )
+
+    first, second = sums[0:2], sums[2:4]
+
+    def both(step, carry):
+        multiply(2 * step, *first)
+        arrange(lax.rem(2 * step + groups - 1, groups), *second)
+        multiply(2 * step + 1, *second)
+        arrange(2 * step, *first)
         return carry
 
-    lax.fori_loop(0, groups, group, 0)
-    out_ref[...] = lax.dot_general(
-        query[...], store_ref[...], LANES_BOTH, preferred_element_type=F32
-    ) * (1.0 / RANK)
+    lax.fori_loop(0, groups // 2, both, 0)
+    arrange(groups - 1, *second)
+
+    result = lax.dot_general(query[...], store_ref[...], LANES_BOTH, preferred_element_type=F32)
+    out_ref[...] = result * (1.0 / RANK)
 
 
 def body(hidden, panel, in_proj, out_proj, targets, keep, span_ids, store):
@@ -127,11 +176,9 @@
     cols = panel.shape[1]
     devices = lax.axis_size("voc")
     share = width // devices
-    base = lax.axis_index("voc") * cols
-    local_span = span_ids - lax.axis_index("tok") * SPAN_DEV
     steps = 4
     piece = width // steps
-    one = lambda i, b: (0, 0)
+    one = lambda i: (0, 0)
     logit, msg, inner = call(
         functools.partial(logits_kernel, steps),
         (
@@ -140,19 +187,19 @@
             jax.ShapeDtypeStruct((RANK + 16, tokens), BF16),
         ),
         grid_spec=pltpu.PrefetchScalarGridSpec(
-            num_scalar_prefetch=1,
+            num_scalar_prefetch=0,
             grid=(steps,),
             in_specs=[
-                pl.BlockSpec((tokens, piece), lambda i, b: (0, i)),
-                pl.BlockSpec((piece, cols), lambda i, b: (i, 0)),
-                pl.BlockSpec((RANK, piece), lambda i, b: (0, i)),
+                pl.BlockSpec((tokens, piece), lambda i: (0, i)),
+                pl.BlockSpec((piece, cols), lambda i: (i, 0)),
+                pl.BlockSpec((RANK, piece), lambda i: (0, i)),
                 pl.BlockSpec((RANK, cols), one),
                 pl.BlockSpec((1, tokens), one),
                 pl.BlockSpec((1, tokens), one),
             ],
             out_specs=[
                 pl.BlockSpec((cols, tokens), one),
-                pl.BlockSpec((devices, 8, tokens), lambda i, b: (0, 0, 0)),
+                pl.BlockSpec((devices, 8, tokens), lambda i: (0, 0, 0)),
                 pl.BlockSpec((RANK + 16, tokens), one),
             ],
             scratch_shapes=[
@@ -162,7 +209,7 @@
             ],
         ),
         name="logits",
-    )(base[None], hidden, panel, in_proj.T, out_proj.T, targets[None], local_span[None])
+    )(hidden, panel, in_proj.T, out_proj.T, targets[None], span_ids[None])
     with jax.named_scope("stats_move"):
         got = lax.all_to_all(msg, "voc", 0, 0, tiled=True)
     with jax.named_scope("inner_move"):
@@ -178,14 +225,25 @@
         out_specs=tuple(vmem(2)),
         scratch_shapes=[pltpu.VMEM((devices, tokens), F32)],
         name="combine",
-    )(got, keep[None])
+    )(resident(got), keep[None])
     with jax.named_scope("outer_move"):
         outer = lax.all_to_all(outer, "voc", 0, 0, tiled=True)
-    with jax.named_scope("grad"):
-        ids = base + lax.broadcasted_iota(jnp.int32, (cols, tokens), 0)
-        onehot = (ids == targets[None]).astype(F32)
-        grad = ((jnp.exp(logit - lse) - onehot) * keep.astype(F32)[None]).astype(BF16)
-        partial = jnp.dot(panel, grad, preferred_element_type=F32).astype(BF16)
+    blocks = 4
+    partial = call(
+        grad_kernel,
+        jax.ShapeDtypeStruct((width, tokens), BF16),
+        grid=(blocks,),
+        in_specs=[
+            pl.BlockSpec((cols, tokens), one),
+            pl.BlockSpec((1, tokens), one),
+            pl.BlockSpec((1, tokens), one),
+            pl.BlockSpec((1, tokens), one),
+            pl.BlockSpec((width // blocks, cols), lambda i: (i, 0)),
+        ],
+        out_specs=pl.BlockSpec((width // blocks, tokens), lambda i: (i, 0)),
+        scratch_shapes=[pltpu.VMEM((cols, tokens), BF16)],
+        name="grad",
+    )(logit, lse, targets[None], keep[None], panel)
     partial = partial.reshape(devices, share, tokens)
     outer, partial = lax.optimization_barrier((outer, partial))
     with jax.named_scope("hidden_move"):
@@ -198,14 +256,18 @@
         jax.ShapeDtypeStruct((groups * SPAN_DEV, store.shape[0]), F32),
         in_specs=vmem(3),
         out_specs=vmem(1)[0],
-        scratch_shapes=[
-            pltpu.VMEM((RANK * 8, tokens), BF16),
-            pltpu.VMEM((RANK * 8, RANK * 4), F32),
-            pltpu.VMEM((groups * SPAN_DEV, RANK * RANK), BF16),
-        ],
+        scratch_shapes=[pltpu.VMEM((groups * SPAN_DEV, RANK * RANK), BF16)]
+        + [pltpu.VMEM((2, RANK, 128), F32)]
+        + [pltpu.VMEM((RANK * 4, RANK * 4), F32)] * 4,
         name="scores",
-    )(all_outer, all_inner, store)
-    hidden_grad = jnp.sum(parts.astype(F32), axis=0).astype(BF16).T
+    )(resident(all_outer), resident(all_inner), resident(store))
+    hidden_grad = call(
+        total_kernel,
+        jax.ShapeDtypeStruct((share, tokens), BF16),
+        in_specs=vmem(1),
+        out_specs=vmem(1)[0],
+        name="total",
+    )(resident(parts)).T
     return (hidden_grad, scores)
 
 

time: 96.7 us -> 94.3 us (0.975)
  the two profiles are of different devices: /device:TPU:1 before, /device:TPU:64 now
where the time goes in v3:
time: 94.3 us; the launch traced here: 93.7 us
  blocking collectives  35.7 us (38%)
  starting transfers between devices  27.2 us (29%)
  waiting for transfers between devices  11.7 us (12%)
  Pallas kernels  11.2 us (12%)
  local copies, waits for them, and re-layouts  7.14 us (8%)
    all_gather x1, blocking collectives, body(): all_inner = lax.all_gather(inner, 'tok', axis=0)  19.4 us
    all_gather x1, blocking collectives, body(): all_outer = lax.all_gather(outer.reshape(RANK, tokens), 'tok', axis=0)  16.4 us
    all_to_all x1, starting transfers between devices, body(): got = lax.all_to_all(msg, 'voc', 0, 0, tiled=True)  12.6 us
    all_to_all x1, starting transfers between devices, body(): outer = lax.all_to_all(outer, 'voc', 0, 0, tiled=True)  9.78 us
    unnamed x20, local copies, waits for them, and re-layouts  7.12 us
    all_to_all x1, waiting for transfers between devices, body(): outer = lax.all_to_all(outer, 'voc', 0, 0, tiled=True)  6.63 us
    all_to_all x1, waiting for transfers between devices, body(): parts = lax.all_to_all(partial, 'voc', 0, 0, tiled=True)  5.06 us
    pallas_call x1, Pallas kernels, body(): call(scores_kernel, jax.ShapeDtypeStruct((groups * SPAN_DEV, store.shape[...  4.97 us
  transfers between devices with their start and end apart: 3, of which 2 were waited for; matrix products, arithmetic and copies ran while one was open for 0% of the time, Pallas kernels for 8%

profile of v3, /device:TPU:64, one launch (start us, length us, event | category | flops | bytes accessed | tf_op | source)
XLA Modules:
  0.0 93.7 jit_solution(9561284103842135736)
XLA Ops:
  0.6 0.0 copy-start.7
  0.6 0.0 copy-start.8
  0.7 0.0 copy-start
  0.7 1.2 %copy-done = bf16[2048,256]{1,0:T(8,128)(2,1)S(1)} copy-done((bf16[2048,256]{1,0:T(8,128)(2,1)S(1)}, bf16[2048,256]{1,0:T(8,128)(2,1)}, u32[]{:S(2)}) %copy-start) | copy-done | bytes 1048600
  1.9 1.2 %copy-done.3 = bf16[256,2048]{1,0:T(8,128)(2,1)S(1)} copy-done((bf16[256,2048]{1,0:T(8,128)(2,1)S(1)}, bf16[256,2048]{1,0:T(8,128)(2,1)}, u32[]{:S(2)}) %copy-start.3) | copy-done | bytes 1048600
  3.1 0.9 %copy-done.4 = bf16[2048,64]{0,1:T(8,128)(2,1)S(1)} copy-done((bf16[2048,64]{0,1:T(8,128)(2,1)S(1)}, bf16[2048,64]{0,1:T(8,128)(2,1)}, u32[]{:S(2)}) %copy-start.4) | copy-done | bytes 262168
  4.1 0.8 copy-done.5
  4.8 0.7 copy-done.6
  5.5 0.7 copy-done.9
  6.2 2.5 %logits.1 = (f32[256,256]{1,0:T(8,128)S(1)}, f32[32,8,256]{2,1,0:T(8,128)}, bf16[80,256]{1,0:T(8,128)(2,1)S(1)}) custom-call(bf16[256,2048]{1,0:T(8,128)(2,1)S(1)} %copy-done.3, bf16[2048,256]{1,0:T(8,128)(2,1)S(1)} %copy-done, bf16[64,2048]{1,0:T(8,128)(2,1)S(1)} %bitcast.9, bf16[64,256]{1,0:T(8,128)(2,1)S(1)} %bitcast.10, s32[1,256]{1,0:T(1,128)S(1)} %bitcast.11, ...), custom_call_target="tpu_custom_call" | custom-call | tf_op jit(solution)/shard_map/logits/pallas_call | solution.py:182
  8.7 12.6 %all-to-all-start = ((f32[32,8,256]{2,1,0:T(8,128)}), f32[32,8,256]{2,1,0:T(8,128)S(1)}, u32[]{:S(2)}, u32[]{:S(2)}) async-start(f32[32,8,256]{2,1,0:T(8,128)} %get-tuple-element.11), calls=%async_computation | async-start | bytes 524288 | tf_op jit(solution)/shard_map/stats_move/all_to_all | solution.py:214
  21.3 19.4 %all-gather = bf16[1280,256]{1,0:T(8,128)(2,1)S(1)} all-gather(bf16[80,256]{1,0:T(8,128)(2,1)S(1)} %get-tuple-element.12), channel_id=2, replica_groups=mesh['tok'=16,'voc'=32] {'tok'}, dimensions={0}, use_global_device_ids=true | all-gather | bytes 696320 | tf_op jit(solution)/shard_map/inner_move/all_gather | solution.py:216
  40.7 0.0 all-to-all-done.got_ref
  40.7 0.0 copy-done.8
  40.7 0.8 combine.1
  41.4 9.8 %all-to-all-start.1 = ((bf16[32,2,256]{2,1,0:T(2,128)(2,1)}), bf16[32,2,256]{2,1,0:T(2,128)(2,1)S(1)}, u32[]{:S(2)}, u32[]{:S(2)}) async-start(bf16[32,2,256]{2,1,0:T(2,128)(2,1)} %get-tuple-element.14), calls=%async_computation.1 | async-start | bytes 65536 | tf_op jit(solution)/shard_map/outer_move/all_to_all | solution.py:230
  51.3 2.2 %grad.1 = bf16[2048,256]{1,0:T(8,128)(2,1)} custom-call(f32[256,256]{1,0:T(8,128)S(1)} %get-tuple-element.15.logit_ref, f32[1,256]{1,0:T(1,128)S(1)} %get-tuple-element.16.lse_ref, s32[1,256]{1,0:T(1,128)S(1)} %bitcast.12, s32[1,256]{1,0:T(1,128)S(1)} %bitcast.14, bf16[2048,256]{1,0:T(8,128)(2,1)S(1)} %copy-done.1), custom_call_target="tpu_custom_call" | custom-call | tf_op jit(solution)/shard_map/grad/pallas_call | solution.py:232
  53.5 6.6 %all-to-all-done.1 = bf16[32,2,256]{2,1,0:T(2,128)(2,1)S(1)} async-done(((bf16[32,2,256]{2,1,0:T(2,128)(2,1)}), bf16[32,2,256]{2,1,0:T(2,128)(2,1)S(1)}, u32[]{:S(2)}, u32[]{:S(2)}) %all-to-all-start.1) | async-done | bytes 32800 | tf_op jit(solution)/shard_map/outer_move/all_to_all | solution.py:230
  60.1 4.8 %all-to-all-start.2 = ((bf16[32,64,256]{2,1,0:T(8,128)(2,1)}), bf16[32,64,256]{2,1,0:T(8,128)(2,1)S(1)}, u32[]{:S(2)}, u32[]{:S(2)}) async-start(bf16[32,64,256]{2,1,0:T(8,128)(2,1)} %bitcast.6), calls=%async_computation.2 | async-start | bytes 2097152 | tf_op jit(solution)/shard_map/hidden_move/all_to_all | solution.py:250
  65.0 16.4 %all_gather.11.outer_ref = bf16[16,64,256]{2,1,0:T(8,128)(2,1)S(1)} all-gather(bf16[1,64,256]{2,1,0:T(8,128)(2,1)S(1)} %reshape.11), channel_id=1, replica_groups=mesh['tok'=16,'voc'=32] {'tok'}, dimensions={0}, use_global_device_ids=true | all-gather | bytes 557056 | tf_op jit(solution)/shard_map/gather_move/all_gather | solution.py:252
  81.3 1.6 %copy-done.2 = bf16[256,4096]{1,0:T(8,128)(2,1)S(1)} copy-done((bf16[256,4096]{1,0:T(8,128)(2,1)S(1)}, bf16[256,4096]{1,0:T(8,128)(2,1)}, u32[]{:S(2)}) %copy-start.2) | copy-done | bytes 2097176
  82.9 5.0 %scores.1 = f32[512,256]{1,0:T(8,128)} custom-call(bf16[16,64,256]{2,1,0:T(8,128)(2,1)S(1)} %all_gather.11.outer_ref, bf16[16,80,256]{2,1,0:T(8,128)(2,1)S(1)} %bitcast.8, bf16[256,4096]{1,0:T(8,128)(2,1)S(1)} %copy-done.2), custom_call_target="tpu_custom_call" | custom-call | tf_op jit(solution)/shard_map/scores/pallas_call | solution.py:254
  87.9 5.1 %all-to-all-done.2.parts_ref = bf16[32,64,256]{2,1,0:T(8,128)(2,1)S(1)} async-done(((bf16[32,64,256]{2,1,0:T(8,128)(2,1)}), bf16[32,64,256]{2,1,0:T(8,128)(2,1)S(1)}, u32[]{:S(2)}, u32[]{:S(2)}) %all-to-all-start.2) | async-done | bytes 1048608 | tf_op jit(solution)/shard_map/hidden_move/all_to_all | solution.py:250
  93.0 0.8 total.1
  (10 shorter events, 0.0 us)
Async XLA Ops:
  0.6 50.6 %copy-start.7 = (s32[256]{0:T(256)S(1)}, s32[256]{0:T(256)}, u32[]{:S(2)}) copy-start(s32[256]{0:T(256)} %param.12) | copy-start | bytes 3076
  0.6 40.0 %copy-start.8 = (s32[256]{0:T(256)S(1)}, s32[256]{0:T(256)}, u32[]{:S(2)}) copy-start(s32[256]{0:T(256)} %param.13) | copy-start | bytes 3076
  0.7 1.2 %copy-start = (bf16[2048,256]{1,0:T(8,128)(2,1)S(1)}, bf16[2048,256]{1,0:T(8,128)(2,1)}, u32[]{:S(2)}) copy-start(bf16[2048,256]{1,0:T(8,128)(2,1)} %pan_ref.3) | copy-start | bytes 3145732
  1.9 1.2 %copy-start.3 = (bf16[256,2048]{1,0:T(8,128)(2,1)S(1)}, bf16[256,2048]{1,0:T(8,128)(2,1)}, u32[]{:S(2)}) copy-start(bf16[256,2048]{1,0:T(8,128)(2,1)} %hid_ref.1) | copy-start | bytes 3145732
  3.1 0.9 %copy-start.4 = (bf16[2048,64]{0,1:T(8,128)(2,1)S(1)}, bf16[2048,64]{0,1:T(8,128)(2,1)}, u32[]{:S(2)}) copy-start(bf16[2048,64]{0,1:T(8,128)(2,1)} %param.10) | copy-start | bytes 786436
  4.1 0.8 copy-start.5
  4.8 0.7 copy-start.6
  5.5 0.7 copy-start.9
  6.2 45.1 %copy-start.1 = (bf16[2048,256]{1,0:T(8,128)(2,1)S(1)}, bf16[2048,256]{1,0:T(8,128)(2,1)}, u32[]{:S(2)}) copy-start(bf16[2048,256]{1,0:T(8,128)(2,1)} %pan_ref.3) | copy-start | bytes 3145732
  8.7 32.0 %all-to-all-start = ((f32[32,8,256]{2,1,0:T(8,128)}), f32[32,8,256]{2,1,0:T(8,128)S(1)}, u32[]{:S(2)}, u32[]{:S(2)}) async-start(f32[32,8,256]{2,1,0:T(8,128)} %get-tuple-element.11), calls=%async_computation | async-start | bytes 524288 | tf_op jit(solution)/shard_map/stats_move/all_to_all | solution.py:214
  41.4 18.6 %all-to-all-start.1 = ((bf16[32,2,256]{2,1,0:T(2,128)(2,1)}), bf16[32,2,256]{2,1,0:T(2,128)(2,1)S(1)}, u32[]{:S(2)}, u32[]{:S(2)}) async-start(bf16[32,2,256]{2,1,0:T(2,128)(2,1)} %get-tuple-element.14), calls=%async_computation.1 | async-start | bytes 65536 | tf_op jit(solution)/shard_map/outer_move/all_to_all | solution.py:230
  60.1 32.9 %all-to-all-start.2 = ((bf16[32,64,256]{2,1,0:T(8,128)(2,1)}), bf16[32,64,256]{2,1,0:T(8,128)(2,1)S(1)}, u32[]{:S(2)}, u32[]{:S(2)}) async-start(bf16[32,64,256]{2,1,0:T(8,128)(2,1)} %bitcast.6), calls=%async_computation.2 | async-start | bytes 2097152 | tf_op jit(solution)/shard_map/hidden_move/all_to_all | solution.py:250
  81.3 1.6 %copy-start.2 = (bf16[256,4096]{1,0:T(8,128)(2,1)S(1)}, bf16[256,4096]{1,0:T(8,128)(2,1)}, u32[]{:S(2)}) copy-start(bf16[256,4096]{1,0:T(8,128)(2,1)} %store_ref.1) | copy-start | bytes 6291460

commit v4 on v3

--- a/solution.py
+++ b/solution.py
@@ -28,70 +28,109 @@
     return [pl.BlockSpec(memory_space=pltpu.VMEM)] * n
 
 
-def logits_kernel(steps, hid_ref, pan_ref, inp_ref, outp_ref, tgt_ref, span_ref,
-                  logit_ref, msg_ref, inner_ref, acc, acc_in, rows):
-    step = pl.program_id(0)
-    part = jnp.dot(hid_ref[...], pan_ref[...], preferred_element_type=F32)
-    part_in = lax.dot_general(inp_ref[...], hid_ref[...], LANES_BOTH, preferred_element_type=F32)
-
-    @pl.when(step == 0)
-    def _():
-        acc[...] = part
-        acc_in[...] = part_in
-
-    @pl.when(step > 0)
-    def _():
-        acc[...] += part
-        acc_in[...] += part_in
-
-    @pl.when(step == steps - 1)
-    def _():
-        tokens = acc.shape[0]
-        inner_ref[0:RANK, :] = acc_in[...].astype(BF16)
-        span = (span_ref[...] - lax.axis_index("tok") * SPAN_DEV).astype(F32)
-        inner_ref[RANK:, :] = jnp.broadcast_to(span, (16, tokens)).astype(BF16)
-        logit = acc[...].T
-        logit_ref[...] = logit
-        cols = lax.broadcasted_iota(jnp.int32, logit.shape, 0)
-        hot = cols == tgt_ref[...] - lax.axis_index("voc") * acc.shape[1]
-        others = jnp.where(hot, LOW, logit)
-        top = jnp.max(others, axis=0, keepdims=True)
-        weight = jnp.exp(others - top)
-        total = jnp.sum(weight, axis=0, keepdims=True)
-        own = jnp.max(jnp.where(hot, logit, LOW), axis=0, keepdims=True)
-        proj = outp_ref[...]
-        rows[0:RANK, :] = jnp.dot(proj, weight.astype(BF16), preferred_element_type=F32)
-        rows[RANK:, :] = jnp.dot(proj, hot.astype(F32).astype(BF16), preferred_element_type=F32)
-        stats = jnp.concatenate([top, total, own], axis=0)
-        devices = msg_ref.shape[0]
-        share = RANK // devices
-        for w in range(devices):
-            msg_ref[w, 0:3, :] = stats
-            msg_ref[w, 3 : 3 + share, :] = rows[share * w : share * (w + 1), :]
-            msg_ref[w, 3 + share : 3 + 2 * share, :] = rows[RANK + share * w : RANK + share * (w + 1), :]
-            msg_ref[w, 3 + 2 * share :, :] = jnp.zeros((5 - 2 * share, tokens), F32)
-
-
-def combine_kernel(got_ref, keep_ref, out_ref, lse_ref, coef):
-    devices = got_ref.shape[0]
-    tops = got_ref[:, 0, :]
-    totals = got_ref[:, 1, :]
-    own = jnp.max(got_ref[:, 2, :], axis=0, keepdims=True)
+def pieces(x, count):
+    found = []
+    for _ in range(count):
+        found.append(x.astype(BF16))
+        x = x - found[-1].astype(F32)
+    return found
+
+
+def logits_kernel(classes, hid_ref, pan_ref, inp_ref, outp_ref, tgt_ref, span_ref,
+                  logit_ref, msg_ref, inner_ref,
+                  hid, pan, inp, outp, tgt, span, acc, acc_in, sems):
+    steps, tokens, piece = hid.shape
+    small = [
+        pltpu.make_async_copy(a, b, sems.at[2 * steps + k])
+        for k, (a, b) in enumerate(((inp_ref, inp), (outp_ref, outp), (tgt_ref, tgt), (span_ref, span)))
+    ]
+    left = [
+        pltpu.make_async_copy(hid_ref.at[:, piece * i : piece * (i + 1)], hid.at[i], sems.at[i])
+        for i in range(steps)
+    ]
+    right = [
+        pltpu.make_async_copy(
+            pan_ref.at[piece * i : piece * (i + 1), :], pan.at[i], sems.at[steps + i]
+        )
+        for i in range(steps)
+    ]
+    for i in range(steps):
+        left[i].start()
+        right[i].start()
+        if i == 0:
+            small[0].start()
+    for copy in small[1:]:
+        copy.start()
+    for i in range(steps):
+        left[i].wait()
+        right[i].wait()
+        if i == 0:
+            small[0].wait()
+        part = jnp.dot(hid[i], pan[i], preferred_element_type=F32)
+        part_in = lax.dot_general(
+            inp[:, piece * i : piece * (i + 1)], hid[i], LANES_BOTH, preferred_element_type=F32
+        )
+        if i == 0:
+            acc[...] = part
+            acc_in[...] = part_in
+        else:
+            acc[...] += part
+            acc_in[...] += part_in
+    for copy in small[1:]:
+        copy.wait()
+    inner_ref[0:RANK, :] = acc_in[...].astype(BF16)
+    local = (span[...] - lax.axis_index("tok") * SPAN_DEV).astype(F32)
+    inner_ref[RANK:, :] = jnp.broadcast_to(local, (16, tokens)).astype(BF16)
+    logit = acc[...].T
+    logit_ref[...] = logit
+    cols = lax.broadcasted_iota(jnp.int32, logit.shape, 0)
+    hot = cols == tgt[...] - lax.axis_index("voc") * logit.shape[0]
+    others = jnp.where(hot, LOW, logit)
+    top = jnp.max(others, axis=0, keepdims=True)
+    weight = jnp.exp(others - top)
+    total = jnp.sum(weight, axis=0, keepdims=True)
+    own = jnp.max(jnp.where(hot, logit, LOW), axis=0, keepdims=True)
+    proj = outp[...]
+    soft = jnp.dot(proj, weight.astype(BF16), preferred_element_type=F32).astype(BF16)
+    picked = jnp.dot(proj, hot.astype(F32).astype(BF16), preferred_element_type=F32).astype(BF16)
+    stats = pieces(top, 3) + pieces(total, 2) + pieces(own, 3)
+    stats = jnp.concatenate([x.astype(F32) for x in stats], axis=0).astype(BF16)
+    devices = msg_ref.shape[0]
+    peers = devices // classes
+    share = RANK // classes
+    for w in range(devices):
+        at = share * (w // peers)
+        msg_ref[w, 0:share, :] = soft[at : at + share, :]
+        msg_ref[w, share : 2 * share, :] = picked[at : at + share, :]
+        msg_ref[w, 2 * share :, :] = stats
+
+
+def combine_kernel(got_ref, keep_ref, out_ref, lse_ref, stat):
+    devices, height, tokens = got_ref.shape
+    share = (height - 8) // 2
+    for v in range(devices):
+        rows = got_ref[v, 2 * share :, :].astype(F32)
+        stat[0, v : v + 1, :] = rows[0:1, :] + rows[1:2, :] + rows[2:3, :]
+        stat[1, v : v + 1, :] = rows[3:4, :] + rows[4:5, :]
+        stat[2, v : v + 1, :] = rows[5:6, :] + rows[6:7, :] + rows[7:8, :]
+    tops = stat[0]
+    own = jnp.max(stat[2], axis=0, keepdims=True)
     top = jnp.maximum(jnp.max(tops, axis=0, keepdims=True), own)
     scale = jnp.exp(tops - top)
-    rest = jnp.sum(scale * totals, axis=0, keepdims=True)
+    rest = jnp.sum(scale * stat[1], axis=0, keepdims=True)
     total = rest + jnp.exp(own - top)
     lse_ref[...] = top + jnp.log(total)
     keep = keep_ref[...].astype(F32)
-    coef[...] = scale * (keep / total)
+    stat[0] = scale * (keep / total)
     gone = keep * (rest / total)
-    part = jnp.zeros((2, top.shape[1]), F32)
-    hot = jnp.zeros((2, top.shape[1]), F32)
+    part = jnp.zeros((share, tokens), F32)
+    hot = jnp.zeros((share, tokens), F32)
     for v in range(devices):
-        part += coef[v : v + 1, :] * got_ref[v, 3:5, :]
-        hot += got_ref[v, 5:7, :]
+        part += stat[0, v : v + 1, :] * got_ref[v, 0:share, :].astype(F32)
+        hot += got_ref[v, share : 2 * share, :].astype(F32)
     outer = (part - gone * hot).astype(BF16)
-    out_ref[...] = jnp.broadcast_to(outer[None], out_ref.shape)
+    for w in range(out_ref.shape[0]):
+        out_ref[w] = outer
 
 
 def grad_kernel(logit_ref, lse_ref, tgt_ref, keep_ref, pan_ref, out_ref, grad):
@@ -115,7 +154,7 @@
     out_ref[...] = total.astype(BF16)
 
 
-def scores_kernel(outer_ref, inner_ref, store_ref, out_ref, query, wide, *sums):
+def scores_kernel(outer_ref, inner_ref, store_hbm, out_ref, query, wide, store_ref, sem, *sums):
     groups, rank, tokens = outer_ref.shape
     half = rank // 2
     low = lax.broadcasted_iota(jnp.int32, (8, 128), 1) < rank
@@ -156,6 +195,8 @@
                 )
 
     first, second = sums[0:2], sums[2:4]
+    fetch = pltpu.make_async_copy(store_hbm, store_ref, sem)
+    fetch.start()
 
     def both(step, carry):
         multiply(2 * step, *first)
@@ -167,6 +208,7 @@
     lax.fori_loop(0, groups // 2, both, 0)
     arrange(groups - 1, *second)
 
+    fetch.wait()
     result = lax.dot_general(query[...], store_ref[...], LANES_BOTH, preferred_element_type=F32)
     out_ref[...] = result * (1.0 / RANK)
 
@@ -178,38 +220,32 @@
     share = width // devices
     steps = 4
     piece = width // steps
+    classes = 4
+    height = 2 * RANK // classes + 8
     one = lambda i: (0, 0)
+    inputs = (hidden, panel, in_proj.T, out_proj.T, targets[None], span_ids[None])
     logit, msg, inner = call(
-        functools.partial(logits_kernel, steps),
+        functools.partial(logits_kernel, classes),
         (
             jax.ShapeDtypeStruct((cols, tokens), F32),
-            jax.ShapeDtypeStruct((devices, 8, tokens), F32),
+            jax.ShapeDtypeStruct((devices, height, tokens), BF16),
             jax.ShapeDtypeStruct((RANK + 16, tokens), BF16),
         ),
-        grid_spec=pltpu.PrefetchScalarGridSpec(
-            num_scalar_prefetch=0,
-            grid=(steps,),
-            in_specs=[
-                pl.BlockSpec((tokens, piece), lambda i: (0, i)),
-                pl.BlockSpec((piece, cols), lambda i: (i, 0)),
-                pl.BlockSpec((RANK, piece), lambda i: (0, i)),
-                pl.BlockSpec((RANK, cols), one),
-                pl.BlockSpec((1, tokens), one),
-                pl.BlockSpec((1, tokens), one),
-            ],
-            out_specs=[
-                pl.BlockSpec((cols, tokens), one),
-                pl.BlockSpec((devices, 8, tokens), lambda i: (0, 0, 0)),
-                pl.BlockSpec((RANK + 16, tokens), one),
-            ],
-            scratch_shapes=[
-                pltpu.VMEM((tokens, cols), F32),
-                pltpu.VMEM((RANK, tokens), F32),
-                pltpu.VMEM((2 * RANK, tokens), F32),
-            ],
-        ),
+        in_specs=[pl.BlockSpec(memory_space=pltpu.HBM)] * 6,
+        out_specs=tuple(vmem(3)),
+        scratch_shapes=[
+            pltpu.VMEM((steps, tokens, piece), BF16),
+            pltpu.VMEM((steps, piece, cols), BF16),
+            pltpu.VMEM((RANK, width), BF16),
+            pltpu.VMEM((RANK, cols), BF16),
+            pltpu.VMEM((1, tokens), jnp.int32),
+            pltpu.VMEM((1, tokens), jnp.int32),
+            pltpu.VMEM((tokens, cols), F32),
+            pltpu.VMEM((RANK, tokens), F32),
+            pltpu.SemaphoreType.DMA((2 * steps + 4,)),
+        ],
         name="logits",
-    )(hidden, panel, in_proj.T, out_proj.T, targets[None], span_ids[None])
+    )(*(pltpu.with_memory_space_constraint(x, pltpu.HBM) for x in inputs))
     with jax.named_scope("stats_move"):
         got = lax.all_to_all(msg, "voc", 0, 0, tiled=True)
     with jax.named_scope("inner_move"):
@@ -218,16 +254,18 @@
     outer, lse = call(
         combine_kernel,
         (
-            jax.ShapeDtypeStruct((devices, 2, tokens), BF16),
+            jax.ShapeDtypeStruct((classes, RANK // classes, tokens), BF16),
             jax.ShapeDtypeStruct((1, tokens), F32),
         ),
         in_specs=vmem(2),
         out_specs=tuple(vmem(2)),
-        scratch_shapes=[pltpu.VMEM((devices, tokens), F32)],
+        scratch_shapes=[pltpu.VMEM((3, devices, tokens), F32)],
         name="combine",
     )(resident(got), keep[None])
     with jax.named_scope("outer_move"):
-        outer = lax.all_to_all(outer, "voc", 0, 0, tiled=True)
+        peers = devices // classes
+        lines = [[z + peers * x for x in range(classes)] for z in range(peers)]
+        outer = lax.all_to_all(outer, "voc", 0, 0, tiled=True, axis_index_groups=lines)
     blocks = 4
     partial = call(
         grad_kernel,
@@ -254,13 +292,14 @@
     scores = call(
         scores_kernel,
         jax.ShapeDtypeStruct((groups * SPAN_DEV, store.shape[0]), F32),
-        in_specs=vmem(3),
+        in_specs=vmem(2) + [pl.BlockSpec(memory_space=pltpu.HBM)],
         out_specs=vmem(1)[0],
         scratch_shapes=[pltpu.VMEM((groups * SPAN_DEV, RANK * RANK), BF16)]
         + [pltpu.VMEM((2, RANK, 128), F32)]
+        + [pltpu.VMEM(store.shape, BF16), pltpu.SemaphoreType.DMA]
         + [pltpu.VMEM((RANK * 4, RANK * 4), F32)] * 4,
         name="scores",
-    )(resident(all_outer), resident(all_inner), resident(store))
+    )(resident(all_outer), resident(all_inner), pltpu.with_memory_space_constraint(store, pltpu.HBM))
     hidden_grad = call(
         total_kernel,
         jax.ShapeDtypeStruct((share, tokens), BF16),

time: 94.3 us -> 83.4 us (0.88)
  local copies, waits for them, and re-layouts: 7.14 us -> 0.01 us
  starting transfers between devices: 27.2 us -> 23.9 us
  waiting for transfers between devices: 11.7 us -> 10.4 us
  Pallas kernels: 11.2 us -> 12.2 us
    unnamed x20 -> x6, local copies, waits for them, and re-layouts: 7.12 us -> 0.01 us
    all_to_all x1, starting transfers between devices: 9.78 us -> 3.36 us  [body(): lax.all_to_all(outer, 'voc', 0, 0, tiled=True, axis_index_groups=lines)]
    all_to_all x1, waiting for transfers between devices: 6.63 us -> 3.24 us  [body(): lax.all_to_all(outer, 'voc', 0, 0, tiled=True, axis_index_groups=lines)]
    all_to_all x1, starting transfers between devices: 4.84 us -> 7.98 us  [body(): parts = lax.all_to_all(partial, 'voc', 0, 0, tiled=True)]
    all_to_all x1, waiting for transfers between devices: 5.06 us -> 6.24 us  [body(): parts = lax.all_to_all(partial, 'voc', 0, 0, tiled=True)]
  transfers between devices with their start and end apart: 3 -> 3, of which waited for: 2 -> 3; matrix products, arithmetic and copies ran while one was open for 0% -> 0% of each run, Pallas kernels for 8% -> 9%
where the time goes in v4:
time: 83.4 us; the launch traced here: 83 us
  blocking collectives  35.7 us (43%)
  starting transfers between devices  23.9 us (29%)
  Pallas kernels  12.2 us (15%)
  waiting for transfers between devices  10.4 us (12%)
    all_gather x1, blocking collectives, body(): all_inner = lax.all_gather(inner, 'tok', axis=0)  19.4 us
    all_gather x1, blocking collectives, body(): all_outer = lax.all_gather(outer.reshape(RANK, tokens), 'tok', axis=0)  16.4 us
    all_to_all x1, starting transfers between devices, body(): got = lax.all_to_all(msg, 'voc', 0, 0, tiled=True)  12.6 us
    all_to_all x1, starting transfers between devices, body(): parts = lax.all_to_all(partial, 'voc', 0, 0, tiled=True)  7.98 us
    all_to_all x1, waiting for transfers between devices, body(): parts = lax.all_to_all(partial, 'voc', 0, 0, tiled=True)  6.24 us
    pallas_call x1, Pallas kernels, body(): call(scores_kernel, jax.ShapeDtypeStruct((groups * SPAN_DEV, store.shape[...  5.09 us
    all_to_all x1, starting transfers between devices, body(): lax.all_to_all(outer, 'voc', 0, 0, tiled=True, axis_index_groups=lines)  3.36 us
    pallas_call x1, Pallas kernels, body(): call(functools.partial(logits_kernel, classes), (jax.ShapeDtypeStruct((co...  3.33 us
  transfers between devices with their start and end apart: 3, of which 3 were waited for; matrix products, arithmetic and copies ran while one was open for 0% of the time, Pallas kernels for 9%

profile of v4, /device:TPU:64, one launch (start us, length us, event | category | flops | bytes accessed | tf_op | source)
XLA Modules:
  0.0 83.0 jit_solution(13914715623202912894)
XLA Ops:
  0.6 0.0 copy-start.2
  0.6 0.0 copy-start
  0.7 0.0 copy-start.1
  0.7 3.3 %logits.1 = (f32[256,256]{1,0:T(8,128)S(1)}, bf16[32,40,256]{2,1,0:T(8,128)(2,1)}, bf16[80,256]{1,0:T(8,128)(2,1)S(1)}) custom-call(bf16[256,2048]{1,0:T(8,128)(2,1)} %hid_ref.1, bf16[2048,256]{1,0:T(8,128)(2,1)} %pan_ref.3, bf16[64,2048]{1,0:T(8,128)(2,1)} %bitcast.14, bf16[64,256]{1,0:T(8,128)(2,1)} %bitcast.16, s32[1,256]{1,0:T(1,128)} %bitcast.10, ...), custom_call_target="tpu_custom_call" | custom-call | tf_op jit(solution)/shard_map/logits/pallas_call | solution.py:227
  4.0 12.6 %all-to-all-start = ((bf16[32,40,256]{2,1,0:T(8,128)(2,1)}), bf16[32,40,256]{2,1,0:T(8,128)(2,1)S(1)}, u32[]{:S(2)}, u32[]{:S(2)}) async-start(bf16[32,40,256]{2,1,0:T(8,128)(2,1)} %get-tuple-element.11), calls=%async_computation | async-start | bytes 1310720 | tf_op jit(solution)/shard_map/stats_move/all_to_all | solution.py:250
  16.6 19.4 %all-gather = bf16[1280,256]{1,0:T(8,128)(2,1)S(1)} all-gather(bf16[80,256]{1,0:T(8,128)(2,1)S(1)} %get-tuple-element.12), channel_id=2, replica_groups=mesh['tok'=16,'voc'=32] {'tok'}, dimensions={0}, use_global_device_ids=true | all-gather | bytes 696320 | tf_op jit(solution)/shard_map/inner_move/all_gather | solution.py:252
  36.0 0.9 %all-to-all-done.got_ref = bf16[32,40,256]{2,1,0:T(8,128)(2,1)S(1)} async-done(((bf16[32,40,256]{2,1,0:T(8,128)(2,1)}), bf16[32,40,256]{2,1,0:T(8,128)(2,1)S(1)}, u32[]{:S(2)}, u32[]{:S(2)}) %all-to-all-start) | async-done | bytes 655392 | tf_op jit(solution)/shard_map/stats_move/all_to_all | solution.py:250
  36.9 0.0 copy-done.2
  36.9 0.8 %combine.1 = (bf16[4,16,256]{2,1,0:T(8,128)(2,1)}, f32[1,256]{1,0:T(1,128)S(1)}) custom-call(bf16[32,40,256]{2,1,0:T(8,128)(2,1)S(1)} %all-to-all-done.got_ref, s32[1,256]{1,0:T(1,128)S(1)} %bitcast.12), custom_call_target="tpu_custom_call" | custom-call | tf_op jit(solution)/shard_map/combine/pallas_call | solution.py:254
  37.7 3.4 %all-to-all-start.1 = ((bf16[4,16,256]{2,1,0:T(8,128)(2,1)}), bf16[4,16,256]{2,1,0:T(8,128)(2,1)S(1)}, u32[]{:S(2)}, u32[]{:S(2)}) async-start(bf16[4,16,256]{2,1,0:T(8,128)(2,1)} %get-tuple-element.14), calls=%async_computation.1 | async-start | bytes 65536 | tf_op jit(solution)/shard_map/outer_move/all_to_all | solution.py:268
  41.1 0.0 copy-done
  41.1 0.0 copy-done.1
  41.1 2.2 %grad.1 = bf16[2048,256]{1,0:T(8,128)(2,1)} custom-call(f32[256,256]{1,0:T(8,128)S(1)} %get-tuple-element.15.logit_ref, f32[1,256]{1,0:T(1,128)S(1)} %get-tuple-element.16.lse_ref, s32[1,256]{1,0:T(1,128)S(1)} %bitcast.11, s32[1,256]{1,0:T(1,128)S(1)} %bitcast.13, bf16[2048,256]{1,0:T(8,128)(2,1)S(1)} %copy-done), custom_call_target="tpu_custom_call" | custom-call | tf_op jit(solution)/shard_map/grad/pallas_call | solution.py:270
  43.3 3.2 %all-to-all-done.1 = bf16[4,16,256]{2,1,0:T(8,128)(2,1)S(1)} async-done(((bf16[4,16,256]{2,1,0:T(8,128)(2,1)}), bf16[4,16,256]{2,1,0:T(8,128)(2,1)S(1)}, u32[]{:S(2)}, u32[]{:S(2)}) %all-to-all-start.1) | async-done | bytes 32800 | tf_op jit(solution)/shard_map/outer_move/all_to_all | solution.py:268
  46.5 8.0 %all-to-all-start.2 = ((bf16[32,64,256]{2,1,0:T(8,128)(2,1)}), bf16[32,64,256]{2,1,0:T(8,128)(2,1)S(1)}, u32[]{:S(2)}, u32[]{:S(2)}) async-start(bf16[32,64,256]{2,1,0:T(8,128)(2,1)} %bitcast.6), calls=%async_computation.2 | async-start | bytes 2097152 | tf_op jit(solution)/shard_map/hidden_move/all_to_all | solution.py:288
  54.5 16.4 %all_gather.11.outer_ref = bf16[16,64,256]{2,1,0:T(8,128)(2,1)S(1)} all-gather(bf16[1,64,256]{2,1,0:T(8,128)(2,1)S(1)} %bitcast.15), channel_id=1, replica_groups=mesh['tok'=16,'voc'=32] {'tok'}, dimensions={0}, use_global_device_ids=true | all-gather | bytes 557056 | tf_op jit(solution)/shard_map/gather_move/all_gather | solution.py:290
  70.9 5.1 %scores.1 = f32[512,256]{1,0:T(8,128)} custom-call(bf16[16,64,256]{2,1,0:T(8,128)(2,1)S(1)} %all_gather.11.outer_ref, bf16[16,80,256]{2,1,0:T(8,128)(2,1)S(1)} %bitcast.9, bf16[256,4096]{1,0:T(8,128)(2,1)} %store_hbm.1), custom_call_target="tpu_custom_call" | custom-call | tf_op jit(solution)/shard_map/scores/pallas_call | solution.py:292
  76.0 6.2 %all-to-all-done.2.parts_ref = bf16[32,64,256]{2,1,0:T(8,128)(2,1)S(1)} async-done(((bf16[32,64,256]{2,1,0:T(8,128)(2,1)}), bf16[32,64,256]{2,1,0:T(8,128)(2,1)S(1)}, u32[]{:S(2)}, u32[]{:S(2)}) %all-to-all-start.2) | async-done | bytes 1048608 | tf_op jit(solution)/shard_map/hidden_move/all_to_all | solution.py:288
  82.2 0.8 total.1
Async XLA Ops:
  0.6 36.2 %copy-start.2 = (s32[256]{0:T(256)S(1)}, s32[256]{0:T(256)}, u32[]{:S(2)}) copy-start(s32[256]{0:T(256)} %param.13) | copy-start | bytes 3076
  0.6 40.4 %copy-start = (bf16[2048,256]{1,0:T(8,128)(2,1)S(1)}, bf16[2048,256]{1,0:T(8,128)(2,1)}, u32[]{:S(2)}) copy-start(bf16[2048,256]{1,0:T(8,128)(2,1)} %pan_ref.3) | copy-start | bytes 3145732
  0.7 40.4 %copy-start.1 = (s32[256]{0:T(256)S(1)}, s32[256]{0:T(256)}, u32[]{:S(2)}) copy-start(s32[256]{0:T(256)} %param.12) | copy-start | bytes 3076
  4.0 32.9 %all-to-all-start = ((bf16[32,40,256]{2,1,0:T(8,128)(2,1)}), bf16[32,40,256]{2,1,0:T(8,128)(2,1)S(1)}, u32[]{:S(2)}, u32[]{:S(2)}) async-start(bf16[32,40,256]{2,1,0:T(8,128)(2,1)} %get-tuple-element.11), calls=%async_computation | async-start | bytes 1310720 | tf_op jit(solution)/shard_map/stats_move/all_to_all | solution.py:250
  37.7 8.8 %all-to-all-start.1 = ((bf16[4,16,256]{2,1,0:T(8,128)(2,1)}), bf16[4,16,256]{2,1,0:T(8,128)(2,1)S(1)}, u32[]{:S(2)}, u32[]{:S(2)}) async-start(bf16[4,16,256]{2,1,0:T(8,128)(2,1)} %get-tuple-element.14), calls=%async_computation.1 | async-start | bytes 65536 | tf_op jit(solution)/shard_map/outer_move/all_to_all | solution.py:268
  46.5 35.7 %all-to-all-start.2 = ((bf16[32,64,256]{2,1,0:T(8,128)(2,1)}), bf16[32,64,256]{2,1,0:T(8,128)(2,1)S(1)}, u32[]{:S(2)}, u32[]{:S(2)}) async-start(bf16[32,64,256]{2,1,0:T(8,128)(2,1)} %bitcast.6), calls=%async_computation.2 | async-start | bytes 2097152 | tf_op jit(solution)/shard_map/hidden_move/all_to_all | solution.py:288

commit v5 on v4

--- a/solution.py
+++ b/solution.py
@@ -105,44 +105,60 @@
         msg_ref[w, 2 * share :, :] = stats
 
 
-def combine_kernel(got_ref, keep_ref, out_ref, lse_ref, stat):
+def combine_kernel(got_ref, logit_ref, tgt_ref, keep_ref, pan_ref, out_ref, stat, grad, chunk):
     devices, height, tokens = got_ref.shape
     share = (height - 8) // 2
-    for v in range(devices):
-        rows = got_ref[v, 2 * share :, :].astype(F32)
-        stat[0, v : v + 1, :] = rows[0:1, :] + rows[1:2, :] + rows[2:3, :]
-        stat[1, v : v + 1, :] = rows[3:4, :] + rows[4:5, :]
-        stat[2, v : v + 1, :] = rows[5:6, :] + rows[6:7, :] + rows[7:8, :]
-    tops = stat[0]
-    own = jnp.max(stat[2], axis=0, keepdims=True)
-    top = jnp.maximum(jnp.max(tops, axis=0, keepdims=True), own)
-    scale = jnp.exp(tops - top)
-    rest = jnp.sum(scale * stat[1], axis=0, keepdims=True)
-    total = rest + jnp.exp(own - top)
-    lse_ref[...] = top + jnp.log(total)
-    keep = keep_ref[...].astype(F32)
-    stat[0] = scale * (keep / total)
-    gone = keep * (rest / total)
-    part = jnp.zeros((share, tokens), F32)
-    hot = jnp.zeros((share, tokens), F32)
-    for v in range(devices):
-        part += stat[0, v : v + 1, :] * got_ref[v, 0:share, :].astype(F32)
-        hot += got_ref[v, share : 2 * share, :].astype(F32)
-    outer = (part - gone * hot).astype(BF16)
-    for w in range(out_ref.shape[0]):
-        out_ref[w] = outer
-
-
-def grad_kernel(logit_ref, lse_ref, tgt_ref, keep_ref, pan_ref, out_ref, grad):
+
     @pl.when(pl.program_id(0) == 0)
     def _():
+        for v in range(devices):
+            rows = got_ref[v, 2 * share :, :].astype(F32)
+            stat[0, v : v + 1, :] = rows[0:1, :] + rows[1:2, :] + rows[2:3, :]
+            stat[1, v : v + 1, :] = rows[3:4, :] + rows[4:5, :]
+            stat[2, v : v + 1, :] = rows[5:6, :] + rows[6:7, :] + rows[7:8, :]
+        tops = stat[0]
+        own = jnp.max(stat[2], axis=0, keepdims=True)
+        top = jnp.maximum(jnp.max(tops, axis=0, keepdims=True), own)
+        scale = jnp.exp(tops - top)
+        rest = jnp.sum(scale * stat[1], axis=0, keepdims=True)
+        total = rest + jnp.exp(own - top)
+        lse = top + jnp.log(total)
+        keep = keep_ref[...].astype(F32)
+        stat[0] = scale * (keep / total)
+        gone = keep * (rest / total)
         cols = lax.broadcasted_iota(jnp.int32, logit_ref.shape, 0)
         hot = cols == tgt_ref[...] - lax.axis_index("voc") * logit_ref.shape[0]
-        soft = jnp.exp(logit_ref[...] - lse_ref[...])
-        keep = keep_ref[...].astype(F32)
+        soft = jnp.exp(logit_ref[...] - lse)
         grad[...] = ((soft - hot.astype(F32)) * keep).astype(BF16)
-
-    out_ref[...] = jnp.dot(pan_ref[...], grad[...], preferred_element_type=F32).astype(BF16)
+        part = jnp.zeros((share, tokens), F32)
+        picked = jnp.zeros((share, tokens), F32)
+        for v in range(devices):
+            part += stat[0, v : v + 1, :] * got_ref[v, 0:share, :].astype(F32)
+            picked += got_ref[v, share : 2 * share, :].astype(F32)
+        chunk[...] = (part - gone * picked).astype(BF16)
+
+    out_ref[0, 0:share, :] = chunk[...]
+    out_ref[0, share:, :] = jnp.dot(
+        pan_ref[...], grad[...], preferred_element_type=F32
+    ).astype(BF16)
+
+
+def line_kernel(got_ref, outer_ref, sum_ref):
+    classes, share, _ = outer_ref.shape
+    for x in range(classes):
+        outer_ref[x] = got_ref[x, 0:share, :]
+    rows = sum_ref.shape[0]
+    step = 64
+
+    def add(k, carry):
+        at = pl.multiple_of(k * step, step)
+        total = got_ref[0, pl.ds(share + at, step), :].astype(F32)
+        for x in range(1, classes):
+            total += got_ref[x, pl.ds(share + at, step), :].astype(F32)
+        sum_ref[pl.ds(at, step), :] = total.astype(BF16)
+        return carry
+
+    lax.fori_loop(0, rows // step, add, 0)
 
 
 def total_kernel(parts_ref, out_ref):
@@ -251,41 +267,45 @@
     with jax.named_scope("inner_move"):
         all_inner = lax.all_gather(inner, "tok", axis=0)
     got, all_inner = lax.optimization_barrier((got, all_inner))
-    outer, lse = call(
+    peers = devices // classes
+    rows = width // classes
+    mixed = call(
         combine_kernel,
-        (
-            jax.ShapeDtypeStruct((classes, RANK // classes, tokens), BF16),
-            jax.ShapeDtypeStruct((1, tokens), F32),
-        ),
-        in_specs=vmem(2),
-        out_specs=tuple(vmem(2)),
-        scratch_shapes=[pltpu.VMEM((3, devices, tokens), F32)],
-        name="combine",
-    )(resident(got), keep[None])
-    with jax.named_scope("outer_move"):
-        peers = devices // classes
-        lines = [[z + peers * x for x in range(classes)] for z in range(peers)]
-        outer = lax.all_to_all(outer, "voc", 0, 0, tiled=True, axis_index_groups=lines)
-    blocks = 4
-    partial = call(
-        grad_kernel,
-        jax.ShapeDtypeStruct((width, tokens), BF16),
-        grid=(blocks,),
+        jax.ShapeDtypeStruct((classes, RANK // classes + rows, tokens), BF16),
+        grid=(classes,),
         in_specs=[
+            pl.BlockSpec((devices, height, tokens), lambda i: (0, 0, 0)),
             pl.BlockSpec((cols, tokens), one),
             pl.BlockSpec((1, tokens), one),
             pl.BlockSpec((1, tokens), one),
-            pl.BlockSpec((1, tokens), one),
-            pl.BlockSpec((width // blocks, cols), lambda i: (i, 0)),
+            pl.BlockSpec((rows, cols), lambda i: (i, 0)),
         ],
-        out_specs=pl.BlockSpec((width // blocks, tokens), lambda i: (i, 0)),
-        scratch_shapes=[pltpu.VMEM((cols, tokens), BF16)],
-        name="grad",
-    )(logit, lse, targets[None], keep[None], panel)
-    partial = partial.reshape(devices, share, tokens)
-    outer, partial = lax.optimization_barrier((outer, partial))
+        out_specs=pl.BlockSpec((1, RANK // classes + rows, tokens), lambda i: (i, 0, 0)),
+        scratch_shapes=[
+            pltpu.VMEM((3, devices, tokens), F32),
+            pltpu.VMEM((cols, tokens), BF16),
+            pltpu.VMEM((RANK // classes, tokens), BF16),
+        ],
+        name="combine",
+    )(resident(got), resident(logit), targets[None], keep[None], resident(panel))
+    with jax.named_scope("mixed_move"):
+        lines = [[z + peers * x for x in range(classes)] for z in range(peers)]
+        mixed = lax.all_to_all(mixed, "voc", 0, 0, tiled=True, axis_index_groups=lines)
+    outer, partial = call(
+        line_kernel,
+        (
+            jax.ShapeDtypeStruct((classes, RANK // classes, tokens), BF16),
+            jax.ShapeDtypeStruct((rows, tokens), BF16),
+        ),
+        in_specs=vmem(1),
+        out_specs=tuple(vmem(2)),
+        name="line",
+    )(resident(mixed))
     with jax.named_scope("hidden_move"):
-        parts = lax.all_to_all(partial, "voc", 0, 0, tiled=True)
+        planes = [[z + peers * x for z in range(peers)] for x in range(classes)]
+        parts = lax.all_to_all(
+            partial.reshape(peers, share, tokens), "voc", 0, 0, tiled=True, axis_index_groups=planes
+        )
     with jax.named_scope("gather_move"):
         all_outer = lax.all_gather(outer.reshape(RANK, tokens), "tok", axis=0)
     groups = all_outer.shape[0]

time: 83.4 us -> 89.6 us (1.074)
  the two profiles are of different devices: /device:TPU:64 before, /device:TPU:1 now
where the time goes in v5:
time: 89.6 us; the launch traced here: 89.2 us
  blocking collectives  57.1 us (64%)
  starting transfers between devices  20.3 us (23%)
  Pallas kernels  11.1 us (12%)
    all_gather x1, blocking collectives, body(): all_inner = lax.all_gather(inner, 'tok', axis=0)  20.2 us
    all_to_all x1, blocking collectives, body(): lax.all_to_all(mixed, 'voc', 0, 0, tiled=True, axis_index_groups=lines)  19.2 us
    all_gather x1, blocking collectives, body(): all_outer = lax.all_gather(outer.reshape(RANK, tokens), 'tok', axis=0)  17.7 us
    all_to_all x1, starting transfers between devices, body(): got = lax.all_to_all(msg, 'voc', 0, 0, tiled=True)  13.8 us
    all_to_all x1, starting transfers between devices, body(): lax.all_to_all(partial.reshape(peers, share, tokens), 'voc', 0, 0, tiled=...  6.41 us
    pallas_call x1, Pallas kernels, body(): call(scores_kernel, jax.ShapeDtypeStruct((groups * SPAN_DEV, store.shape[...  5.09 us
    pallas_call x1, Pallas kernels, body(): call(functools.partial(logits_kernel, classes), (jax.ShapeDtypeStruct((co...  3.23 us
  transfers between devices with their start and end apart: 2, of which 0 were waited for; matrix products, arithmetic and copies ran while one was open for 0% of the time, Pallas kernels for 6%

profile of v5, /device:TPU:1, one launch (start us, length us, event | category | flops | bytes accessed | tf_op | source)
XLA Modules:
  0.0 89.2 jit_solution(480629300444927078)
XLA Ops:
  0.6 3.2 %logits.1 = (f32[256,256]{1,0:T(8,128)S(1)}, bf16[32,40,256]{2,1,0:T(8,128)(2,1)}, bf16[80,256]{1,0:T(8,128)(2,1)S(1)}) custom-call(bf16[256,2048]{1,0:T(8,128)(2,1)} %hid_ref.1, bf16[2048,256]{1,0:T(8,128)(2,1)} %pan_ref.3, bf16[64,2048]{1,0:T(8,128)(2,1)} %bitcast.14, bf16[64,256]{1,0:T(8,128)(2,1)} %bitcast.15, s32[1,256]{1,0:T(1,128)} %bitcast.11, ...), custom_call_target="tpu_custom_call" | custom-call | tf_op jit(solution)/shard_map/logits/pallas_call | solution.py:243
  3.9 0.0 copy-start
  3.9 0.0 copy-start.1
  3.9 0.0 copy-start.2
  3.9 13.8 %all-to-all-start = ((bf16[32,40,256]{2,1,0:T(8,128)(2,1)}), bf16[32,40,256]{2,1,0:T(8,128)(2,1)S(1)}, u32[]{:S(2)}, u32[]{:S(2)}) async-start(bf16[32,40,256]{2,1,0:T(8,128)(2,1)} %get-tuple-element.9), calls=%async_computation | async-start | bytes 1310720 | tf_op jit(solution)/shard_map/stats_move/all_to_all | solution.py:266
  17.8 20.2 %all-gather = bf16[1280,256]{1,0:T(8,128)(2,1)S(1)} all-gather(bf16[80,256]{1,0:T(8,128)(2,1)S(1)} %get-tuple-element.10), channel_id=2, replica_groups=mesh['tok'=16,'voc'=32] {'tok'}, dimensions={0}, use_global_device_ids=true | all-gather | bytes 696320 | tf_op jit(solution)/shard_map/inner_move/all_gather | solution.py:268
  37.9 0.0 all-to-all-done.got_ref
  37.9 0.0 copy-done
  37.9 0.0 copy-done.1
  37.9 0.0 copy-done.2
  38.0 1.3 %combine.1 = bf16[4,528,256]{2,1,0:T(8,128)(2,1)S(1)} custom-call(bf16[32,40,256]{2,1,0:T(8,128)(2,1)S(1)} %all-to-all-done.got_ref, f32[256,256]{1,0:T(8,128)S(1)} %get-tuple-element.12.logit_ref, s32[1,256]{1,0:T(1,128)S(1)} %bitcast.12, s32[1,256]{1,0:T(1,128)S(1)} %bitcast.13, bf16[2048,256]{1,0:T(8,128)(2,1)S(1)} %copy-done), custom_call_target="tpu_custom_call" | custom-call | tf_op jit(solution)/shard_map/combine/pallas_call | solution.py:272
  39.2 19.2 %all_to_all.15.got_ref = bf16[4,528,256]{2,1,0:T(8,128)(2,1)S(1)} all-to-all(bf16[4,528,256]{2,1,0:T(8,128)(2,1)S(1)} %combine.1), channel_id=1, replica_groups={{0,8,16,24},{1,9,17,25},{2,10,18,26},{3,11,19,27},{4,12,20,28},{5,13,21..., dimensions={0} | all-to-all | bytes 2162688 | tf_op jit(solution)/shard_map/mixed_move/all_to_all | solution.py:293
  58.4 0.9 line.1
  59.3 6.4 %all-to-all-start.2 = ((bf16[8,64,256]{2,1,0:T(8,128)(2,1)}), bf16[8,64,256]{2,1,0:T(8,128)(2,1)S(1)}, u32[]{:S(2)}, u32[]{:S(2)}) async-start(bf16[8,64,256]{2,1,0:T(8,128)(2,1)} %bitcast.6), calls=%async_computation.2 | async-start | bytes 524288 | tf_op jit(solution)/shard_map/hidden_move/all_to_all | solution.py:306
  65.7 17.7 %all_gather.11.outer_ref = bf16[16,64,256]{2,1,0:T(8,128)(2,1)S(1)} all-gather(bf16[1,64,256]{2,1,0:T(8,128)(2,1)S(1)} %bitcast.10), channel_id=1, replica_groups=mesh['tok'=16,'voc'=32] {'tok'}, dimensions={0}, use_global_device_ids=true | all-gather | bytes 557056 | tf_op jit(solution)/shard_map/gather_move/all_gather | solution.py:310
  83.4 5.1 %scores.1 = f32[512,256]{1,0:T(8,128)} custom-call(bf16[16,64,256]{2,1,0:T(8,128)(2,1)S(1)} %all_gather.11.outer_ref, bf16[16,80,256]{2,1,0:T(8,128)(2,1)S(1)} %bitcast.9, bf16[256,4096]{1,0:T(8,128)(2,1)} %store_hbm.1), custom_call_target="tpu_custom_call" | custom-call | tf_op jit(solution)/shard_map/scores/pallas_call | solution.py:312
  88.5 0.0 all-to-all-done.2.parts_ref
  88.5 0.7 total.1
Async XLA Ops:
  3.9 34.1 %copy-start = (bf16[2048,256]{1,0:T(8,128)(2,1)S(1)}, bf16[2048,256]{1,0:T(8,128)(2,1)}, u32[]{:S(2)}) copy-start(bf16[2048,256]{1,0:T(8,128)(2,1)} %pan_ref.3) | copy-start | bytes 3145732
  3.9 34.1 %copy-start.1 = (s32[256]{0:T(256)S(1)}, s32[256]{0:T(256)}, u32[]{:S(2)}) copy-start(s32[256]{0:T(256)} %param.12) | copy-start | bytes 3076
  3.9 34.1 %copy-start.2 = (s32[256]{0:T(256)S(1)}, s32[256]{0:T(256)}, u32[]{:S(2)}) copy-start(s32[256]{0:T(256)} %param.13) | copy-start | bytes 3076
  3.9 34.0 %all-to-all-start = ((bf16[32,40,256]{2,1,0:T(8,128)(2,1)}), bf16[32,40,256]{2,1,0:T(8,128)(2,1)S(1)}, u32[]{:S(2)}, u32[]{:S(2)}) async-start(bf16[32,40,256]{2,1,0:T(8,128)(2,1)} %get-tuple-element.9), calls=%async_computation | async-start | bytes 1310720 | tf_op jit(solution)/shard_map/stats_move/all_to_all | solution.py:266
  59.3 29.3 %all-to-all-start.2 = ((bf16[8,64,256]{2,1,0:T(8,128)(2,1)}), bf16[8,64,256]{2,1,0:T(8,128)(2,1)S(1)}, u32[]{:S(2)}, u32[]{:S(2)}) async-start(bf16[8,64,256]{2,1,0:T(8,128)(2,1)} %bitcast.6), calls=%async_computation.2 | async-start | bytes 524288 | tf_op jit(solution)/shard_map/hidden_move/all_to_all | solution.py:306

commit v6 on v4

--- a/solution.py
+++ b/solution.py
@@ -6,6 +6,7 @@
 from jax.experimental import pallas as pl
 from jax.experimental.pallas import tpu as pltpu
 from jax.sharding import PartitionSpec as P
+
 
 RANK = 64
 SPAN_DEV = 32
@@ -80,7 +81,7 @@
         copy.wait()
     inner_ref[0:RANK, :] = acc_in[...].astype(BF16)
     local = (span[...] - lax.axis_index("tok") * SPAN_DEV).astype(F32)
-    inner_ref[RANK:, :] = jnp.broadcast_to(local, (16, tokens)).astype(BF16)
+    inner_ref[RANK:, :] = jnp.broadcast_to(local, (8, tokens)).astype(BF16)
     logit = acc[...].T
     logit_ref[...] = logit
     cols = lax.broadcasted_iota(jnp.int32, logit.shape, 0)
@@ -129,8 +130,7 @@
         part += stat[0, v : v + 1, :] * got_ref[v, 0:share, :].astype(F32)
         hot += got_ref[v, share : 2 * share, :].astype(F32)
     outer = (part - gone * hot).astype(BF16)
-    for w in range(out_ref.shape[0]):
-        out_ref[w] = outer
+    out_ref[...] = outer
 
 
 def grad_kernel(logit_ref, lse_ref, tgt_ref, keep_ref, pan_ref, out_ref, grad):
@@ -142,7 +142,24 @@
         keep = keep_ref[...].astype(F32)
         grad[...] = ((soft - hot.astype(F32)) * keep).astype(BF16)
 
-    out_ref[...] = jnp.dot(pan_ref[...], grad[...], preferred_element_type=F32).astype(BF16)
+    rows = out_ref.shape[0]
+    at = pl.multiple_of(pl.program_id(0) * rows, rows)
+    out_ref[...] = jnp.dot(
+        pan_ref[pl.ds(at, rows), :], grad[...], preferred_element_type=F32
+    ).astype(BF16)
+
+
+def pair_kernel(own_ref, near_ref, out_ref):
+    out_ref[0] = own_ref[...]
+    out_ref[1] = near_ref[...]
+
+
+def assemble_kernel(pair_ref, far_ref, out_ref):
+    mine = lax.axis_index("voc") // 8
+    out_ref[mine] = pair_ref[0]
+    out_ref[mine ^ 1] = pair_ref[1]
+    out_ref[mine ^ 3] = far_ref[0]
+    out_ref[mine ^ 2] = far_ref[1]
 
 
 def total_kernel(parts_ref, out_ref):
@@ -163,21 +180,24 @@
     def multiply(k, even_ref, odd_ref):
         span = inner_ref[k, rank:, :].astype(F32)
         block = jnp.floor(span * 0.125)
-        row = (span - 8.0 * block)[0:8, :]
+        row = span - 8.0 * block
         mask = (row == eight).astype(F32)
+        mask = jnp.concatenate([mask, mask], axis=0).astype(BF16)
         for c in (0, 1):
             wide[c] = inner_ref[k, 0:rank, 128 * c : 128 * (c + 1)].astype(F32)
         outer = outer_ref[k]
         shares = []
         for j in range(4):
-            chosen = (block == float(j)).astype(F32).astype(BF16)
+            chosen = (block == float(j)).astype(F32)
+            chosen = jnp.concatenate([chosen, chosen], axis=0).astype(BF16)
             shares.append(outer * jnp.concatenate([chosen] * (rank // 16), axis=0))
         for ref, side, order in ((even_ref, 0, (0, 1, 2, 3)), (odd_ref, 1, (1, 0, 3, 2))):
             columns = []
             for c in (0, 1):
                 part = mask[:, 128 * c : 128 * (c + 1)]
-                rows = [wide[c, pl.ds(2 * p + side, 8, stride=0), :] * part for p in range(half)]
-                columns.append(jnp.concatenate(rows, axis=0).astype(BF16))
+                rows = [wide[c, pl.ds(2 * p + side, 8, stride=0), :] for p in range(half)]
+                pairs = [jnp.concatenate(rows[p : p + 2], axis=0).astype(BF16) for p in range(0, half, 2)]
+                columns.append(jnp.concatenate([x * part for x in pairs], axis=0))
             left = jnp.concatenate(columns, axis=1)
             right = jnp.concatenate([shares[j] for j in order], axis=0)
             ref[...] = lax.dot_general(left, right, LANES_BOTH, preferred_element_type=F32)
@@ -199,13 +219,13 @@
     fetch.start()
 
     def both(step, carry):
-        multiply(2 * step, *first)
-        arrange(lax.rem(2 * step + groups - 1, groups), *second)
-        multiply(2 * step + 1, *second)
-        arrange(2 * step, *first)
+        for k in range(4):
+            now, before = (first, second) if k % 2 == 0 else (second, first)
+            multiply(4 * step + k, *now)
+            arrange(lax.rem(4 * step + k + groups - 1, groups), *before)
         return carry
 
-    lax.fori_loop(0, groups // 2, both, 0)
+    lax.fori_loop(0, groups // 4, both, 0)
     arrange(groups - 1, *second)
 
     fetch.wait()
@@ -222,14 +242,13 @@
     piece = width // steps
     classes = 4
     height = 2 * RANK // classes + 8
-    one = lambda i: (0, 0)
     inputs = (hidden, panel, in_proj.T, out_proj.T, targets[None], span_ids[None])
     logit, msg, inner = call(
         functools.partial(logits_kernel, classes),
         (
             jax.ShapeDtypeStruct((cols, tokens), F32),
             jax.ShapeDtypeStruct((devices, height, tokens), BF16),
-            jax.ShapeDtypeStruct((RANK + 16, tokens), BF16),
+            jax.ShapeDtypeStruct((RANK + 8, tokens), BF16),
         ),
         in_specs=[pl.BlockSpec(memory_space=pltpu.HBM)] * 6,
         out_specs=tuple(vmem(3)),
@@ -246,15 +265,13 @@
         ],
         name="logits",
     )(*(pltpu.with_memory_space_constraint(x, pltpu.HBM) for x in inputs))
-    with jax.named_scope("stats_move"):
-        got = lax.all_to_all(msg, "voc", 0, 0, tiled=True)
-    with jax.named_scope("inner_move"):
-        all_inner = lax.all_gather(inner, "tok", axis=0)
+    got = lax.all_to_all(msg, "voc", 0, 0, tiled=True)
+    all_inner = lax.all_gather(inner, "tok", axis=0)
     got, all_inner = lax.optimization_barrier((got, all_inner))
     outer, lse = call(
         combine_kernel,
         (
-            jax.ShapeDtypeStruct((classes, RANK // classes, tokens), BF16),
+            jax.ShapeDtypeStruct((RANK // classes, tokens), BF16),
             jax.ShapeDtypeStruct((1, tokens), F32),
         ),
         in_specs=vmem(2),
@@ -262,32 +279,35 @@
         scratch_shapes=[pltpu.VMEM((3, devices, tokens), F32)],
         name="combine",
     )(resident(got), keep[None])
-    with jax.named_scope("outer_move"):
-        peers = devices // classes
-        lines = [[z + peers * x for x in range(classes)] for z in range(peers)]
-        outer = lax.all_to_all(outer, "voc", 0, 0, tiled=True, axis_index_groups=lines)
+    near = lax.ppermute(outer, "voc", [(v, v ^ 8) for v in range(devices)])
     blocks = 4
     partial = call(
         grad_kernel,
         jax.ShapeDtypeStruct((width, tokens), BF16),
         grid=(blocks,),
-        in_specs=[
-            pl.BlockSpec((cols, tokens), one),
-            pl.BlockSpec((1, tokens), one),
-            pl.BlockSpec((1, tokens), one),
-            pl.BlockSpec((1, tokens), one),
-            pl.BlockSpec((width // blocks, cols), lambda i: (i, 0)),
-        ],
+        in_specs=vmem(5),
         out_specs=pl.BlockSpec((width // blocks, tokens), lambda i: (i, 0)),
         scratch_shapes=[pltpu.VMEM((cols, tokens), BF16)],
         name="grad",
-    )(logit, lse, targets[None], keep[None], panel)
+    )(resident(logit), resident(lse), targets[None], keep[None], resident(panel))
     partial = partial.reshape(devices, share, tokens)
-    outer, partial = lax.optimization_barrier((outer, partial))
-    with jax.named_scope("hidden_move"):
-        parts = lax.all_to_all(partial, "voc", 0, 0, tiled=True)
-    with jax.named_scope("gather_move"):
-        all_outer = lax.all_gather(outer.reshape(RANK, tokens), "tok", axis=0)
+    parts = lax.all_to_all(partial, "voc", 0, 0, tiled=True)
+    pair = call(
+        pair_kernel,
+        jax.ShapeDtypeStruct((2, RANK // classes, tokens), BF16),
+        in_specs=vmem(2),
+        out_specs=vmem(1)[0],
+        name="pair",
+    )(resident(outer), resident(near))
+    far = lax.ppermute(pair, "voc", [(v, v ^ 24) for v in range(devices)])
+    outer = call(
+        assemble_kernel,
+        jax.ShapeDtypeStruct((classes, RANK // classes, tokens), BF16),
+        in_specs=vmem(2),
+        out_specs=vmem(1)[0],
+        name="assemble",
+    )(resident(pair), resident(far))
+    all_outer = lax.all_gather(outer.reshape(RANK, tokens), "tok", axis=0)
     groups = all_outer.shape[0]
     scores = call(
         scores_kernel,
@@ -321,6 +341,7 @@
         P("tok"),
         P(("tok", "voc"), None),
     )
+
     return jax.shard_map(
         body,
         mesh=mesh,

time: 83.4 us -> 84.2 us (level)
  the two profiles are of different devices: /device:TPU:64 before, /device:TPU:1 now
where the time goes in v6:
time: 84.2 us; the launch traced here: 83.8 us
  blocking collectives  37.7 us (45%)
  starting transfers between devices  30.9 us (37%)
  Pallas kernels  10.8 us (13%)
  waiting for transfers between devices  3.71 us (4%)
    all_gather x1, blocking collectives, body(): all_inner = lax.all_gather(inner, 'tok', axis=0)  20 us
    all_gather x1, blocking collectives, body(): all_outer = lax.all_gather(outer.reshape(RANK, tokens), 'tok', axis=0)  17.7 us
    all_to_all x1, starting transfers between devices, body(): got = lax.all_to_all(msg, 'voc', 0, 0, tiled=True)  13.7 us
    all_to_all x1, starting transfers between devices, body(): parts = lax.all_to_all(partial, 'voc', 0, 0, tiled=True)  9.49 us
    ppermute x1, starting transfers between devices, body(): far = lax.ppermute(pair, 'voc', [(v, v ^ 24) for v in range(devices)])  4.51 us
    pallas_call x1, Pallas kernels, body(): call(scores_kernel, jax.ShapeDtypeStruct((groups * SPAN_DEV, store.shape[...  4.25 us
    pallas_call x1, Pallas kernels, body(): call(functools.partial(logits_kernel, classes), (jax.ShapeDtypeStruct((co...  3.32 us
    ppermute x1, starting transfers between devices, body(): near = lax.ppermute(outer, 'voc', [(v, v ^ 8) for v in range(devices)])  3.14 us
  transfers between devices with their start and end apart: 4, of which 2 were waited for; matrix products, arithmetic and copies ran while one was open for 0% of the time, Pallas kernels for 5%

profile of v6, /device:TPU:1, one launch (start us, length us, event | category | flops | bytes accessed | tf_op | source)
XLA Modules:
  0.0 83.8 jit_solution(4876510713515558440)
XLA Ops:
  0.6 0.0 copy-start.2
  0.6 0.0 copy-start
  0.7 0.0 copy-start.1
  0.7 3.3 %logits.1 = (f32[256,256]{1,0:T(8,128)S(1)}, bf16[32,40,256]{2,1,0:T(8,128)(2,1)}, bf16[72,256]{1,0:T(8,128)(2,1)S(1)}) custom-call(bf16[256,2048]{1,0:T(8,128)(2,1)} %hid_ref.1, bf16[2048,256]{1,0:T(8,128)(2,1)} %pan_ref.3, bf16[64,2048]{1,0:T(8,128)(2,1)} %bitcast.15, bf16[64,256]{1,0:T(8,128)(2,1)} %bitcast.16, s32[1,256]{1,0:T(1,128)} %bitcast.11, ...), custom_call_target="tpu_custom_call" | custom-call | tf_op jit(solution)/shard_map/logits/pallas_call | solution.py:246
  4.0 13.7 %all-to-all-start = ((bf16[32,40,256]{2,1,0:T(8,128)(2,1)}), bf16[32,40,256]{2,1,0:T(8,128)(2,1)S(1)}, u32[]{:S(2)}, u32[]{:S(2)}) async-start(bf16[32,40,256]{2,1,0:T(8,128)(2,1)} %get-tuple-element.10), calls=%async_computation | async-start | bytes 1310720 | tf_op jit(solution)/shard_map/all_to_all | solution.py:268
  17.7 20.0 %all-gather = bf16[1152,256]{1,0:T(8,128)(2,1)S(1)} all-gather(bf16[72,256]{1,0:T(8,128)(2,1)S(1)} %get-tuple-element.11), channel_id=2, replica_groups=mesh['tok'=16,'voc'=32] {'tok'}, dimensions={0}, use_global_device_ids=true | all-gather | bytes 626688 | tf_op jit(solution)/shard_map/all_gather | solution.py:269
  37.7 0.0 all-to-all-done.got_ref
  37.7 0.0 copy-done.2
  37.7 0.2 combine.1
  37.9 0.0 copy-done
  37.9 0.0 copy-done.1
  38.0 2.2 %grad.1 = bf16[2048,256]{1,0:T(8,128)(2,1)} custom-call(f32[256,256]{1,0:T(8,128)S(1)} %get-tuple-element.9.logit_ref, f32[1,256]{1,0:T(1,128)S(1)} %get-tuple-element.13.lse_ref, s32[1,256]{1,0:T(1,128)S(1)} %bitcast.12, s32[1,256]{1,0:T(1,128)S(1)} %bitcast.14, bf16[2048,256]{1,0:T(8,128)(2,1)S(1)} %copy-done), custom_call_target="tpu_custom_call" | custom-call | tf_op jit(solution)/shard_map/grad/pallas_call | solution.py:284
  40.2 9.5 %all-to-all-start.1 = ((bf16[32,64,256]{2,1,0:T(8,128)(2,1)}), bf16[32,64,256]{2,1,0:T(8,128)(2,1)S(1)}, u32[]{:S(2)}, u32[]{:S(2)}) async-start(bf16[32,64,256]{2,1,0:T(8,128)(2,1)} %bitcast.6), calls=%async_computation.1 | async-start | bytes 2097152 | tf_op jit(solution)/shard_map/all_to_all | solution.py:294
  49.7 3.1 %collective-permute-start = (bf16[16,256]{1,0:T(8,128)(2,1)S(1)}, bf16[16,256]{1,0:T(8,128)(2,1)S(1)}, u32[]{:S(2)}, u32[]{:S(2)}) collective-permute-start(bf16[16,256]{1,0:T(8,128)(2,1)S(1)} %get-tuple-element.14.own_ref), channel_id=1, source_target_pairs={{0,8},{1,9},{2,10},{3,11},{4,12},{5,13},{6,14},{7,15},{8,0},{9,1},... | collective-permute-start | bytes 24584 | tf_op jit(solution)/shard_map/ppermute | solution.py:282
  52.8 1.5 %collective-permute-done.near_ref = bf16[16,256]{1,0:T(8,128)(2,1)S(1)} collective-permute-done((bf16[16,256]{1,0:T(8,128)(2,1)S(1)}, bf16[16,256]{1,0:T(8,128)(2,1)S(1)}, u32[]{:S(2)}, u32[]{:S(2)}) %collective-permute-start) | collective-permute-done | bytes 8224 | tf_op jit(solution)/shard_map/ppermute | solution.py:282
  54.4 4.5 %collective-permute-start.1 = (bf16[2,16,256]{2,1,0:T(8,128)(2,1)S(1)}, bf16[2,16,256]{2,1,0:T(8,128)(2,1)S(1)}, u32[]{:S(2)}, u32[]{:S(2)}) collective-permute-start(bf16[2,16,256]{2,1,0:T(8,128)(2,1)S(1)} %pair.1.pair_ref), channel_id=1, source_target_pairs={{0,24},{1,25},{2,26},{3,27},{4,28},{5,29},{6,30},{7,31},{8,16},{9,... | collective-permute-start | bytes 49160 | tf_op jit(solution)/shard_map/ppermute | solution.py:302
  58.9 2.2 %collective-permute-done.1.far_ref = bf16[2,16,256]{2,1,0:T(8,128)(2,1)S(1)} collective-permute-done((bf16[2,16,256]{2,1,0:T(8,128)(2,1)S(1)}, bf16[2,16,256]{2,1,0:T(8,128)(2,1)S(1)}, u32[]{:S(2)}, u32[]{:S(2)}) %collective-permute-start.1) | collective-permute-done | bytes 16416 | tf_op jit(solution)/shard_map/ppermute | solution.py:302
  61.0 17.7 %all_gather.11.outer_ref = bf16[16,64,256]{2,1,0:T(8,128)(2,1)S(1)} all-gather(bf16[1,64,256]{2,1,0:T(8,128)(2,1)S(1)} %bitcast.10), channel_id=1, replica_groups=mesh['tok'=16,'voc'=32] {'tok'}, dimensions={0}, use_global_device_ids=true | all-gather | bytes 557056 | tf_op jit(solution)/shard_map/all_gather | solution.py:310
  78.8 4.2 %scores.1 = f32[512,256]{1,0:T(8,128)} custom-call(bf16[16,64,256]{2,1,0:T(8,128)(2,1)S(1)} %all_gather.11.outer_ref, bf16[16,72,256]{2,1,0:T(8,128)(2,1)S(1)} %bitcast.9, bf16[256,4096]{1,0:T(8,128)(2,1)} %store_hbm.1), custom_call_target="tpu_custom_call" | custom-call | tf_op jit(solution)/shard_map/scores/pallas_call | solution.py:312
  83.0 0.0 all-to-all-done.1.parts_ref
  83.1 0.8 total.1
  (2 shorter events, 0.0 us)
Async XLA Ops:
  0.6 37.1 %copy-start.2 = (s32[256]{0:T(256)S(1)}, s32[256]{0:T(256)}, u32[]{:S(2)}) copy-start(s32[256]{0:T(256)} %param.13) | copy-start | bytes 3076
  0.6 37.3 %copy-start = (bf16[2048,256]{1,0:T(8,128)(2,1)S(1)}, bf16[2048,256]{1,0:T(8,128)(2,1)}, u32[]{:S(2)}) copy-start(bf16[2048,256]{1,0:T(8,128)(2,1)} %pan_ref.3) | copy-start | bytes 3145732
  0.7 37.3 %copy-start.1 = (s32[256]{0:T(256)S(1)}, s32[256]{0:T(256)}, u32[]{:S(2)}) copy-start(s32[256]{0:T(256)} %param.12) | copy-start | bytes 3076
  4.0 33.7 %all-to-all-start = ((bf16[32,40,256]{2,1,0:T(8,128)(2,1)}), bf16[32,40,256]{2,1,0:T(8,128)(2,1)S(1)}, u32[]{:S(2)}, u32[]{:S(2)}) async-start(bf16[32,40,256]{2,1,0:T(8,128)(2,1)} %get-tuple-element.10), calls=%async_computation | async-start | bytes 1310720 | tf_op jit(solution)/shard_map/all_to_all | solution.py:268
  40.2 42.9 %all-to-all-start.1 = ((bf16[32,64,256]{2,1,0:T(8,128)(2,1)}), bf16[32,64,256]{2,1,0:T(8,128)(2,1)S(1)}, u32[]{:S(2)}, u32[]{:S(2)}) async-start(bf16[32,64,256]{2,1,0:T(8,128)(2,1)} %bitcast.6), calls=%async_computation.1 | async-start | bytes 2097152 | tf_op jit(solution)/shard_map/all_to_all | solution.py:294
  49.7 4.7 %collective-permute-start = (bf16[16,256]{1,0:T(8,128)(2,1)S(1)}, bf16[16,256]{1,0:T(8,128)(2,1)S(1)}, u32[]{:S(2)}, u32[]{:S(2)}) collective-permute-start(bf16[16,256]{1,0:T(8,128)(2,1)S(1)} %get-tuple-element.14.own_ref), channel_id=1, source_target_pairs={{0,8},{1,9},{2,10},{3,11},{4,12},{5,13},{6,14},{7,15},{8,0},{9,1},... | collective-permute-start | bytes 24584 | tf_op jit(solution)/shard_map/ppermute | solution.py:282
  54.4 6.7 %collective-permute-start.1 = (bf16[2,16,256]{2,1,0:T(8,128)(2,1)S(1)}, bf16[2,16,256]{2,1,0:T(8,128)(2,1)S(1)}, u32[]{:S(2)}, u32[]{:S(2)}) collective-permute-start(bf16[2,16,256]{2,1,0:T(8,128)(2,1)S(1)} %pair.1.pair_ref), channel_id=1, source_target_pairs={{0,24},{1,25},{2,26},{3,27},{4,28},{5,29},{6,30},{7,31},{8,16},{9,... | collective-permute-start | bytes 49160 | tf_op jit(solution)/shard_map/ppermute | solution.py:302

commit v7 on v6

--- a/solution.py
+++ b/solution.py
@@ -133,20 +133,22 @@
     out_ref[...] = outer
 
 
-def grad_kernel(logit_ref, lse_ref, tgt_ref, keep_ref, pan_ref, out_ref, grad):
-    @pl.when(pl.program_id(0) == 0)
-    def _():
-        cols = lax.broadcasted_iota(jnp.int32, logit_ref.shape, 0)
-        hot = cols == tgt_ref[...] - lax.axis_index("voc") * logit_ref.shape[0]
-        soft = jnp.exp(logit_ref[...] - lse_ref[...])
-        keep = keep_ref[...].astype(F32)
-        grad[...] = ((soft - hot.astype(F32)) * keep).astype(BF16)
-
-    rows = out_ref.shape[0]
-    at = pl.multiple_of(pl.program_id(0) * rows, rows)
-    out_ref[...] = jnp.dot(
-        pan_ref[pl.ds(at, rows), :], grad[...], preferred_element_type=F32
-    ).astype(BF16)
+def grad_kernel(logit_ref, lse_ref, tgt_ref, keep_ref, pan_ref, out_ref, made, sems):
+    cols = lax.broadcasted_iota(jnp.int32, logit_ref.shape, 0)
+    hot = cols == tgt_ref[...] - lax.axis_index("voc") * logit_ref.shape[0]
+    soft = jnp.exp(logit_ref[...] - lse_ref[...])
+    keep = keep_ref[...].astype(F32)
+    grad = ((soft - hot.astype(F32)) * keep).astype(BF16)
+    blocks = sems.shape[0]
+    rows = made.shape[0] // blocks
+    copies = []
+    for i in range(blocks):
+        at = slice(rows * i, rows * (i + 1))
+        made[at, :] = jnp.dot(pan_ref[at, :], grad, preferred_element_type=F32).astype(BF16)
+        copies.append(pltpu.make_async_copy(made.at[at, :], out_ref.at[at, :], sems.at[i]))
+        copies[-1].start()
+    for copy in copies:
+        copy.wait()
 
 
 def pair_kernel(own_ref, near_ref, out_ref):
@@ -219,13 +221,13 @@
     fetch.start()
 
     def both(step, carry):
-        for k in range(4):
+        for k in range(8):
             now, before = (first, second) if k % 2 == 0 else (second, first)
-            multiply(4 * step + k, *now)
-            arrange(lax.rem(4 * step + k + groups - 1, groups), *before)
+            multiply(8 * step + k, *now)
+            arrange(lax.rem(8 * step + k + groups - 1, groups), *before)
         return carry
 
-    lax.fori_loop(0, groups // 4, both, 0)
+    lax.fori_loop(0, groups // 8, both, 0)
     arrange(groups - 1, *second)
 
     fetch.wait()
@@ -280,14 +282,15 @@
         name="combine",
     )(resident(got), keep[None])
     near = lax.ppermute(outer, "voc", [(v, v ^ 8) for v in range(devices)])
-    blocks = 4
     partial = call(
         grad_kernel,
         jax.ShapeDtypeStruct((width, tokens), BF16),
-        grid=(blocks,),
         in_specs=vmem(5),
-        out_specs=pl.BlockSpec((width // blocks, tokens), lambda i: (i, 0)),
-        scratch_shapes=[pltpu.VMEM((cols, tokens), BF16)],
+        out_specs=pl.BlockSpec(memory_space=pltpu.HBM),
+        scratch_shapes=[
+            pltpu.VMEM((width, tokens), BF16),
+            pltpu.SemaphoreType.DMA((8,)),
+        ],
         name="grad",
     )(resident(logit), resident(lse), targets[None], keep[None], resident(panel))
     partial = partial.reshape(devices, share, tokens)

time: 84.2 us -> 83.1 us (0.987)
  Pallas kernels: 10.8 us -> 9.65 us
    pallas_call x1, Pallas kernels: 2.21 us -> 1.33 us  [body(): call(grad_kernel, jax.ShapeDtypeStruct((width, tokens), BF16), in_specs=v...]
where the time goes in v7:
time: 83.1 us; the launch traced here: 82.7 us
  blocking collectives  38.4 us (46%)
  starting transfers between devices  30.9 us (37%)
  Pallas kernels  9.65 us (12%)
  waiting for transfers between devices  3.08 us (4%)
    all_gather x1, blocking collectives, body(): all_inner = lax.all_gather(inner, 'tok', axis=0)  20 us
    all_gather x1, blocking collectives, body(): all_outer = lax.all_gather(outer.reshape(RANK, tokens), 'tok', axis=0)  18.4 us
    all_to_all x1, starting transfers between devices, body(): got = lax.all_to_all(msg, 'voc', 0, 0, tiled=True)  13.7 us
    all_to_all x1, starting transfers between devices, body(): parts = lax.all_to_all(partial, 'voc', 0, 0, tiled=True)  9.51 us
    ppermute x1, starting transfers between devices, body(): far = lax.ppermute(pair, 'voc', [(v, v ^ 24) for v in range(devices)])  4.5 us
    pallas_call x1, Pallas kernels, body(): call(scores_kernel, jax.ShapeDtypeStruct((groups * SPAN_DEV, store.shape[...  3.98 us
    pallas_call x1, Pallas kernels, body(): call(functools.partial(logits_kernel, classes), (jax.ShapeDtypeStruct((co...  3.32 us
    ppermute x1, starting transfers between devices, body(): near = lax.ppermute(outer, 'voc', [(v, v ^ 8) for v in range(devices)])  3.14 us
  transfers between devices with their start and end apart: 4, of which 2 were waited for; matrix products, arithmetic and copies ran while one was open for 0% of the time, Pallas kernels for 5%

profile of v7, /device:TPU:1, one launch (start us, length us, event | category | flops | bytes accessed | tf_op | source)
XLA Modules:
  0.0 82.7 jit_solution(9430984751215193257)
XLA Ops:
  0.6 0.0 copy-start.2
  0.6 0.0 copy-start
  0.7 0.0 copy-start.1
  0.7 3.3 %logits.1 = (f32[256,256]{1,0:T(8,128)S(1)}, bf16[32,40,256]{2,1,0:T(8,128)(2,1)}, bf16[72,256]{1,0:T(8,128)(2,1)S(1)}) custom-call(bf16[256,2048]{1,0:T(8,128)(2,1)} %hid_ref.1, bf16[2048,256]{1,0:T(8,128)(2,1)} %pan_ref.3, bf16[64,2048]{1,0:T(8,128)(2,1)} %bitcast.15, bf16[64,256]{1,0:T(8,128)(2,1)} %bitcast.16, s32[1,256]{1,0:T(1,128)} %bitcast.11, ...), custom_call_target="tpu_custom_call" | custom-call | tf_op jit(solution)/shard_map/logits/pallas_call | solution.py:248
  4.0 13.7 %all-to-all-start = ((bf16[32,40,256]{2,1,0:T(8,128)(2,1)}), bf16[32,40,256]{2,1,0:T(8,128)(2,1)S(1)}, u32[]{:S(2)}, u32[]{:S(2)}) async-start(bf16[32,40,256]{2,1,0:T(8,128)(2,1)} %get-tuple-element.10), calls=%async_computation | async-start | bytes 1310720 | tf_op jit(solution)/shard_map/all_to_all | solution.py:270
  17.7 20.0 %all-gather = bf16[1152,256]{1,0:T(8,128)(2,1)S(1)} all-gather(bf16[72,256]{1,0:T(8,128)(2,1)S(1)} %get-tuple-element.11), channel_id=2, replica_groups=mesh['tok'=16,'voc'=32] {'tok'}, dimensions={0}, use_global_device_ids=true | all-gather | bytes 626688 | tf_op jit(solution)/shard_map/all_gather | solution.py:271
  37.7 0.0 all-to-all-done.got_ref
  37.7 0.0 copy-done.2
  37.7 0.2 combine.1
  37.9 0.0 copy-done
  37.9 0.0 copy-done.1
  38.0 1.3 %grad.1 = bf16[2048,256]{1,0:T(8,128)(2,1)} custom-call(f32[256,256]{1,0:T(8,128)S(1)} %get-tuple-element.9.logit_ref, f32[1,256]{1,0:T(1,128)S(1)} %get-tuple-element.13.lse_ref, s32[1,256]{1,0:T(1,128)S(1)} %bitcast.12, s32[1,256]{1,0:T(1,128)S(1)} %bitcast.14, bf16[2048,256]{1,0:T(8,128)(2,1)S(1)} %copy-done), custom_call_target="tpu_custom_call" | custom-call | tf_op jit(solution)/shard_map/grad/pallas_call | solution.py:285
  39.3 9.5 %all-to-all-start.1 = ((bf16[32,64,256]{2,1,0:T(8,128)(2,1)}), bf16[32,64,256]{2,1,0:T(8,128)(2,1)S(1)}, u32[]{:S(2)}, u32[]{:S(2)}) async-start(bf16[32,64,256]{2,1,0:T(8,128)(2,1)} %bitcast.6), calls=%async_computation.1 | async-start | bytes 2097152 | tf_op jit(solution)/shard_map/all_to_all | solution.py:297
  48.8 3.1 %collective-permute-start = (bf16[16,256]{1,0:T(8,128)(2,1)S(1)}, bf16[16,256]{1,0:T(8,128)(2,1)S(1)}, u32[]{:S(2)}, u32[]{:S(2)}) collective-permute-start(bf16[16,256]{1,0:T(8,128)(2,1)S(1)} %get-tuple-element.14.own_ref), channel_id=1, source_target_pairs={{0,8},{1,9},{2,10},{3,11},{4,12},{5,13},{6,14},{7,15},{8,0},{9,1},... | collective-permute-start | bytes 24584 | tf_op jit(solution)/shard_map/ppermute | solution.py:284
  52.0 1.5 %collective-permute-done.near_ref = bf16[16,256]{1,0:T(8,128)(2,1)S(1)} collective-permute-done((bf16[16,256]{1,0:T(8,128)(2,1)S(1)}, bf16[16,256]{1,0:T(8,128)(2,1)S(1)}, u32[]{:S(2)}, u32[]{:S(2)}) %collective-permute-start) | collective-permute-done | bytes 8224 | tf_op jit(solution)/shard_map/ppermute | solution.py:284
  53.5 4.5 %collective-permute-start.1 = (bf16[2,16,256]{2,1,0:T(8,128)(2,1)S(1)}, bf16[2,16,256]{2,1,0:T(8,128)(2,1)S(1)}, u32[]{:S(2)}, u32[]{:S(2)}) collective-permute-start(bf16[2,16,256]{2,1,0:T(8,128)(2,1)S(1)} %pair.1.pair_ref), channel_id=1, source_target_pairs={{0,24},{1,25},{2,26},{3,27},{4,28},{5,29},{6,30},{7,31},{8,16},{9,... | collective-permute-start | bytes 49160 | tf_op jit(solution)/shard_map/ppermute | solution.py:305
  58.0 1.5 %collective-permute-done.1.far_ref = bf16[2,16,256]{2,1,0:T(8,128)(2,1)S(1)} collective-permute-done((bf16[2,16,256]{2,1,0:T(8,128)(2,1)S(1)}, bf16[2,16,256]{2,1,0:T(8,128)(2,1)S(1)}, u32[]{:S(2)}, u32[]{:S(2)}) %collective-permute-start.1) | collective-permute-done | bytes 16416 | tf_op jit(solution)/shard_map/ppermute | solution.py:305
  59.6 18.4 %all_gather.11.outer_ref = bf16[16,64,256]{2,1,0:T(8,128)(2,1)S(1)} all-gather(bf16[1,64,256]{2,1,0:T(8,128)(2,1)S(1)} %bitcast.10), channel_id=1, replica_groups=mesh['tok'=16,'voc'=32] {'tok'}, dimensions={0}, use_global_device_ids=true | all-gather | bytes 557056 | tf_op jit(solution)/shard_map/all_gather | solution.py:313
  77.9 4.0 %scores.1 = f32[512,256]{1,0:T(8,128)} custom-call(bf16[16,64,256]{2,1,0:T(8,128)(2,1)S(1)} %all_gather.11.outer_ref, bf16[16,72,256]{2,1,0:T(8,128)(2,1)S(1)} %bitcast.9, bf16[256,4096]{1,0:T(8,128)(2,1)} %store_hbm.1), custom_call_target="tpu_custom_call" | custom-call | tf_op jit(solution)/shard_map/scores/pallas_call | solution.py:315
  81.9 0.0 all-to-all-done.1.parts_ref
  81.9 0.8 total.1
  (2 shorter events, 0.0 us)
Async XLA Ops:
  0.6 37.1 %copy-start.2 = (s32[256]{0:T(256)S(1)}, s32[256]{0:T(256)}, u32[]{:S(2)}) copy-start(s32[256]{0:T(256)} %param.13) | copy-start | bytes 3076
  0.6 37.3 %copy-start = (bf16[2048,256]{1,0:T(8,128)(2,1)S(1)}, bf16[2048,256]{1,0:T(8,128)(2,1)}, u32[]{:S(2)}) copy-start(bf16[2048,256]{1,0:T(8,128)(2,1)} %pan_ref.3) | copy-start | bytes 3145732
  0.7 37.3 %copy-start.1 = (s32[256]{0:T(256)S(1)}, s32[256]{0:T(256)}, u32[]{:S(2)}) copy-start(s32[256]{0:T(256)} %param.12) | copy-start | bytes 3076
  4.0 33.7 %all-to-all-start = ((bf16[32,40,256]{2,1,0:T(8,128)(2,1)}), bf16[32,40,256]{2,1,0:T(8,128)(2,1)S(1)}, u32[]{:S(2)}, u32[]{:S(2)}) async-start(bf16[32,40,256]{2,1,0:T(8,128)(2,1)} %get-tuple-element.10), calls=%async_computation | async-start | bytes 1310720 | tf_op jit(solution)/shard_map/all_to_all | solution.py:270
  39.3 42.6 %all-to-all-start.1 = ((bf16[32,64,256]{2,1,0:T(8,128)(2,1)}), bf16[32,64,256]{2,1,0:T(8,128)(2,1)S(1)}, u32[]{:S(2)}, u32[]{:S(2)}) async-start(bf16[32,64,256]{2,1,0:T(8,128)(2,1)} %bitcast.6), calls=%async_computation.1 | async-start | bytes 2097152 | tf_op jit(solution)/shard_map/all_to_all | solution.py:297
  48.8 4.7 %collective-permute-start = (bf16[16,256]{1,0:T(8,128)(2,1)S(1)}, bf16[16,256]{1,0:T(8,128)(2,1)S(1)}, u32[]{:S(2)}, u32[]{:S(2)}) collective-permute-start(bf16[16,256]{1,0:T(8,128)(2,1)S(1)} %get-tuple-element.14.own_ref), channel_id=1, source_target_pairs={{0,8},{1,9},{2,10},{3,11},{4,12},{5,13},{6,14},{7,15},{8,0},{9,1},... | collective-permute-start | bytes 24584 | tf_op jit(solution)/shard_map/ppermute | solution.py:284
  53.5 6.0 %collective-permute-start.1 = (bf16[2,16,256]{2,1,0:T(8,128)(2,1)S(1)}, bf16[2,16,256]{2,1,0:T(8,128)(2,1)S(1)}, u32[]{:S(2)}, u32[]{:S(2)}) collective-permute-start(bf16[2,16,256]{2,1,0:T(8,128)(2,1)S(1)} %pair.1.pair_ref), channel_id=1, source_target_pairs={{0,24},{1,25},{2,26},{3,27},{4,28},{5,29},{6,30},{7,31},{8,16},{9,... | collective-permute-start | bytes 49160 | tf_op jit(solution)/shard_map/ppermute | solution.py:305

commit v8 on v7

--- a/solution.py
+++ b/solution.py
@@ -97,10 +97,9 @@
     stats = pieces(top, 3) + pieces(total, 2) + pieces(own, 3)
     stats = jnp.concatenate([x.astype(F32) for x in stats], axis=0).astype(BF16)
     devices = msg_ref.shape[0]
-    peers = devices // classes
     share = RANK // classes
     for w in range(devices):
-        at = share * (w // peers)
+        at = share * (w % classes)
         msg_ref[w, 0:share, :] = soft[at : at + share, :]
         msg_ref[w, share : 2 * share, :] = picked[at : at + share, :]
         msg_ref[w, 2 * share :, :] = stats
@@ -267,7 +266,9 @@
         ],
         name="logits",
     )(*(pltpu.with_memory_space_constraint(x, pltpu.HBM) for x in inputs))
-    got = lax.all_to_all(msg, "voc", 0, 0, tiled=True)
+    peers = devices // classes
+    everyone = [[z + peers * x for z in range(peers) for x in range(classes)]]
+    got = lax.all_to_all(msg, "voc", 0, 0, tiled=True, axis_index_groups=everyone)
     all_inner = lax.all_gather(inner, "tok", axis=0)
     got, all_inner = lax.optimization_barrier((got, all_inner))
     outer, lse = call(

time: 83.1 us -> 83.1 us (level)
  no operation moved by 1% of the time
where the time goes in v8:
time: 83.1 us; the launch traced here: 82.7 us
  blocking collectives  38.4 us (46%)
  starting transfers between devices  30.9 us (37%)
  Pallas kernels  9.65 us (12%)
  waiting for transfers between devices  3.08 us (4%)
    all_gather x1, blocking collectives, body(): all_inner = lax.all_gather(inner, 'tok', axis=0)  20 us
    all_gather x1, blocking collectives, body(): all_outer = lax.all_gather(outer.reshape(RANK, tokens), 'tok', axis=0)  18.4 us
    all_to_all x1, starting transfers between devices, body(): lax.all_to_all(msg, 'voc', 0, 0, tiled=True, axis_index_groups=everyone)  13.7 us
    all_to_all x1, starting transfers between devices, body(): parts = lax.all_to_all(partial, 'voc', 0, 0, tiled=True)  9.51 us
    ppermute x1, starting transfers between devices, body(): far = lax.ppermute(pair, 'voc', [(v, v ^ 24) for v in range(devices)])  4.5 us
    pallas_call x1, Pallas kernels, body(): call(scores_kernel, jax.ShapeDtypeStruct((groups * SPAN_DEV, store.shape[...  3.98 us
    pallas_call x1, Pallas kernels, body(): call(functools.partial(logits_kernel, classes), (jax.ShapeDtypeStruct((co...  3.33 us
    ppermute x1, starting transfers between devices, body(): near = lax.ppermute(outer, 'voc', [(v, v ^ 8) for v in range(devices)])  3.14 us
  transfers between devices with their start and end apart: 4, of which 2 were waited for; matrix products, arithmetic and copies ran while one was open for 0% of the time, Pallas kernels for 5%

profile of v8, /device:TPU:1, one launch (start us, length us, event | category | flops | bytes accessed | tf_op | source)
XLA Modules:
  0.0 82.7 jit_solution(1334273693195623222)
XLA Ops:
  0.6 0.0 copy-start.2
  0.6 0.0 copy-start
  0.7 0.0 copy-start.1
  0.7 3.3 %logits.1 = (f32[256,256]{1,0:T(8,128)S(1)}, bf16[32,40,256]{2,1,0:T(8,128)(2,1)}, bf16[72,256]{1,0:T(8,128)(2,1)S(1)}) custom-call(bf16[256,2048]{1,0:T(8,128)(2,1)} %hid_ref.1, bf16[2048,256]{1,0:T(8,128)(2,1)} %pan_ref.3, bf16[64,2048]{1,0:T(8,128)(2,1)} %bitcast.15, bf16[64,256]{1,0:T(8,128)(2,1)} %bitcast.16, s32[1,256]{1,0:T(1,128)} %bitcast.11, ...), custom_call_target="tpu_custom_call" | custom-call | tf_op jit(solution)/shard_map/logits/pallas_call | solution.py:247
  4.0 13.7 %all-to-all-start = ((bf16[32,40,256]{2,1,0:T(8,128)(2,1)}), bf16[32,40,256]{2,1,0:T(8,128)(2,1)S(1)}, u32[]{:S(2)}, u32[]{:S(2)}) async-start(bf16[32,40,256]{2,1,0:T(8,128)(2,1)} %get-tuple-element.10), calls=%async_computation | async-start | bytes 1310720 | tf_op jit(solution)/shard_map/all_to_all | solution.py:271
  17.7 20.0 %all-gather = bf16[1152,256]{1,0:T(8,128)(2,1)S(1)} all-gather(bf16[72,256]{1,0:T(8,128)(2,1)S(1)} %get-tuple-element.11), channel_id=2, replica_groups=mesh['tok'=16,'voc'=32] {'tok'}, dimensions={0}, use_global_device_ids=true | all-gather | bytes 626688 | tf_op jit(solution)/shard_map/all_gather | solution.py:272
  37.7 0.0 all-to-all-done.got_ref
  37.7 0.0 copy-done.2
  37.7 0.2 combine.1
  37.9 0.0 copy-done
  38.0 0.0 copy-done.1
  38.0 1.3 %grad.1 = bf16[2048,256]{1,0:T(8,128)(2,1)} custom-call(f32[256,256]{1,0:T(8,128)S(1)} %get-tuple-element.9.logit_ref, f32[1,256]{1,0:T(1,128)S(1)} %get-tuple-element.13.lse_ref, s32[1,256]{1,0:T(1,128)S(1)} %bitcast.12, s32[1,256]{1,0:T(1,128)S(1)} %bitcast.14, bf16[2048,256]{1,0:T(8,128)(2,1)S(1)} %copy-done), custom_call_target="tpu_custom_call" | custom-call | tf_op jit(solution)/shard_map/grad/pallas_call | solution.py:286
  39.3 9.5 %all-to-all-start.1 = ((bf16[32,64,256]{2,1,0:T(8,128)(2,1)}), bf16[32,64,256]{2,1,0:T(8,128)(2,1)S(1)}, u32[]{:S(2)}, u32[]{:S(2)}) async-start(bf16[32,64,256]{2,1,0:T(8,128)(2,1)} %bitcast.6), calls=%async_computation.1 | async-start | bytes 2097152 | tf_op jit(solution)/shard_map/all_to_all | solution.py:298
  48.8 3.1 %collective-permute-start = (bf16[16,256]{1,0:T(8,128)(2,1)S(1)}, bf16[16,256]{1,0:T(8,128)(2,1)S(1)}, u32[]{:S(2)}, u32[]{:S(2)}) collective-permute-start(bf16[16,256]{1,0:T(8,128)(2,1)S(1)} %get-tuple-element.14.own_ref), channel_id=1, source_target_pairs={{0,8},{1,9},{2,10},{3,11},{4,12},{5,13},{6,14},{7,15},{8,0},{9,1},... | collective-permute-start | bytes 24584 | tf_op jit(solution)/shard_map/ppermute | solution.py:285
  52.0 1.5 %collective-permute-done.near_ref = bf16[16,256]{1,0:T(8,128)(2,1)S(1)} collective-permute-done((bf16[16,256]{1,0:T(8,128)(2,1)S(1)}, bf16[16,256]{1,0:T(8,128)(2,1)S(1)}, u32[]{:S(2)}, u32[]{:S(2)}) %collective-permute-start) | collective-permute-done | bytes 8224 | tf_op jit(solution)/shard_map/ppermute | solution.py:285
  53.5 4.5 %collective-permute-start.1 = (bf16[2,16,256]{2,1,0:T(8,128)(2,1)S(1)}, bf16[2,16,256]{2,1,0:T(8,128)(2,1)S(1)}, u32[]{:S(2)}, u32[]{:S(2)}) collective-permute-start(bf16[2,16,256]{2,1,0:T(8,128)(2,1)S(1)} %pair.1.pair_ref), channel_id=1, source_target_pairs={{0,24},{1,25},{2,26},{3,27},{4,28},{5,29},{6,30},{7,31},{8,16},{9,... | collective-permute-start | bytes 49160 | tf_op jit(solution)/shard_map/ppermute | solution.py:306
  58.0 1.5 %collective-permute-done.1.far_ref = bf16[2,16,256]{2,1,0:T(8,128)(2,1)S(1)} collective-permute-done((bf16[2,16,256]{2,1,0:T(8,128)(2,1)S(1)}, bf16[2,16,256]{2,1,0:T(8,128)(2,1)S(1)}, u32[]{:S(2)}, u32[]{:S(2)}) %collective-permute-start.1) | collective-permute-done | bytes 16416 | tf_op jit(solution)/shard_map/ppermute | solution.py:306
  59.6 18.4 %all_gather.11.outer_ref = bf16[16,64,256]{2,1,0:T(8,128)(2,1)S(1)} all-gather(bf16[1,64,256]{2,1,0:T(8,128)(2,1)S(1)} %bitcast.10), channel_id=1, replica_groups=mesh['tok'=16,'voc'=32] {'tok'}, dimensions={0}, use_global_device_ids=true | all-gather | bytes 557056 | tf_op jit(solution)/shard_map/all_gather | solution.py:314
  77.9 4.0 %scores.1 = f32[512,256]{1,0:T(8,128)} custom-call(bf16[16,64,256]{2,1,0:T(8,128)(2,1)S(1)} %all_gather.11.outer_ref, bf16[16,72,256]{2,1,0:T(8,128)(2,1)S(1)} %bitcast.9, bf16[256,4096]{1,0:T(8,128)(2,1)} %store_hbm.1), custom_call_target="tpu_custom_call" | custom-call | tf_op jit(solution)/shard_map/scores/pallas_call | solution.py:316
  81.9 0.0 all-to-all-done.1.parts_ref
  81.9 0.8 total.1
  (2 shorter events, 0.0 us)
Async XLA Ops:
  0.6 37.1 %copy-start.2 = (s32[256]{0:T(256)S(1)}, s32[256]{0:T(256)}, u32[]{:S(2)}) copy-start(s32[256]{0:T(256)} %param.13) | copy-start | bytes 3076
  0.6 37.3 %copy-start = (bf16[2048,256]{1,0:T(8,128)(2,1)S(1)}, bf16[2048,256]{1,0:T(8,128)(2,1)}, u32[]{:S(2)}) copy-start(bf16[2048,256]{1,0:T(8,128)(2,1)} %pan_ref.3) | copy-start | bytes 3145732
  0.7 37.3 %copy-start.1 = (s32[256]{0:T(256)S(1)}, s32[256]{0:T(256)}, u32[]{:S(2)}) copy-start(s32[256]{0:T(256)} %param.12) | copy-start | bytes 3076
  4.0 33.7 %all-to-all-start = ((bf16[32,40,256]{2,1,0:T(8,128)(2,1)}), bf16[32,40,256]{2,1,0:T(8,128)(2,1)S(1)}, u32[]{:S(2)}, u32[]{:S(2)}) async-start(bf16[32,40,256]{2,1,0:T(8,128)(2,1)} %get-tuple-element.10), calls=%async_computation | async-start | bytes 1310720 | tf_op jit(solution)/shard_map/all_to_all | solution.py:271
  39.3 42.6 %all-to-all-start.1 = ((bf16[32,64,256]{2,1,0:T(8,128)(2,1)}), bf16[32,64,256]{2,1,0:T(8,128)(2,1)S(1)}, u32[]{:S(2)}, u32[]{:S(2)}) async-start(bf16[32,64,256]{2,1,0:T(8,128)(2,1)} %bitcast.6), calls=%async_computation.1 | async-start | bytes 2097152 | tf_op jit(solution)/shard_map/all_to_all | solution.py:298
  48.8 4.7 %collective-permute-start = (bf16[16,256]{1,0:T(8,128)(2,1)S(1)}, bf16[16,256]{1,0:T(8,128)(2,1)S(1)}, u32[]{:S(2)}, u32[]{:S(2)}) collective-permute-start(bf16[16,256]{1,0:T(8,128)(2,1)S(1)} %get-tuple-element.14.own_ref), channel_id=1, source_target_pairs={{0,8},{1,9},{2,10},{3,11},{4,12},{5,13},{6,14},{7,15},{8,0},{9,1},... | collective-permute-start | bytes 24584 | tf_op jit(solution)/shard_map/ppermute | solution.py:285
  53.5 6.0 %collective-permute-start.1 = (bf16[2,16,256]{2,1,0:T(8,128)(2,1)S(1)}, bf16[2,16,256]{2,1,0:T(8,128)(2,1)S(1)}, u32[]{:S(2)}, u32[]{:S(2)}) collective-permute-start(bf16[2,16,256]{2,1,0:T(8,128)(2,1)S(1)} %pair.1.pair_ref), channel_id=1, source_target_pairs={{0,24},{1,25},{2,26},{3,27},{4,28},{5,29},{6,30},{7,31},{8,16},{9,... | collective-permute-start | bytes 49160 | tf_op jit(solution)/shard_map/ppermute | solution.py:306
